TPU v7x, 256 devices: a whole 4x4x8 slice. The times are simulated.
256 devices in a mesh: row: 16 (over y, x), col: 16 (over z, core).
Axes of the slice: x: 4, y: 4, z: 8, core: 2. Of those that a mesh axis runs over, the one named last changes fastest.
Arguments:
- factor_diag: float32 [2, 512, 512], replicated, as said below
- factor_mid: float32 [512, 512], replicated, may hold values from -0.25 to 0.25
- factor_low: float32 [2, 16384, 512], P(None, ('row', 'col')), may hold values from -0.046875 to 0.046875
- adjoint_diag: float32 [2, 512, 512], replicated, may hold values from -6 to 6
- adjoint_mid: float32 [512, 512], replicated, may hold values from -6 to 6
- adjoint_low: float32 [2, 16384, 512], P(None, ('row', 'col')), may hold values from -6 to 6
- trailing_adjoint: float32 [16384, 16, 1024], P('row', None, 'col'), as said below
Outputs:
- grad_diag: float32 [2, 512, 512], replicated
- grad_mid: float32 [512, 512], replicated
- grad_low: float32 [2, 16384, 512], P(None, ('row', 'col'))
Inputs may be any that keep to these rules, and one draw needn't show every extreme that they name: `factor_diag`: each of the two [512, 512] blocks is lower triangular with diagonal entries between 1 and 2. `trailing_adjoint`: symmetric when read as an 16384 x 16384 matrix in row-major order.
All inputs are finite; a program needn't handle non-finite values.
Results may differ from a plain program's by a relative error of at most 0.000065.
Values sent between devices are 32-bit elements; how exact they have to be, the bound alone decides.
No kernel may reach another device: no remote copies, remote signals or barrier semaphores. Data moves between devices by JAX's collectives and lax.ppermute only.
A program may use at most 128 MiB of HBM per device.

v0:
```python
import jax
import jax.numpy as jnp
from jax import lax
from jax.sharding import PartitionSpec as P


def lower_half(matrix):
    return jnp.tril(matrix, -1) + 0.5 * jnp.diag(jnp.diag(matrix))


def product(left_side, right_side):
    return jnp.dot(
        left_side, right_side, precision=lax.Precision.HIGHEST, preferred_element_type=jnp.float32
    )


def right_solve(factor, row_block):
    return jax.scipy.linalg.solve_triangular(factor, row_block.T, trans=1, lower=True).T


def diag_adjoint(factor, adjoint):
    inner_term = lower_half(product(factor.T, adjoint))
    halfway = jax.scipy.linalg.solve_triangular(factor, inner_term, trans=1, lower=True)
    whole_term = right_solve(factor, halfway)
    return 0.5 * (whole_term + whole_term.T)


def shards(
    factor_diag, factor_mid, factor_low, adjoint_diag, adjoint_mid, adjoint_low, trailing_adjoint
):
    block_rows, row_groups, group_cols = trailing_adjoint.shape
    local_block = trailing_adjoint.reshape(block_rows, row_groups * group_cols)

    def image_of(panel):
        columns = lax.all_gather(panel, "row", axis=0, tiled=True)
        return lax.psum_scatter(
            product(local_block, columns), "col", scatter_dimension=0, tiled=True
        )

    second_image = image_of(factor_low[1])
    first_image = image_of(factor_low[0])
    second_solved = right_solve(factor_diag[1], adjoint_low[1] - 2.0 * second_image)
    second_total = lax.psum(product(second_solved.T, factor_low[1]), ("row", "col"))
    second_grad = diag_adjoint(factor_diag[1], adjoint_diag[1] - second_total)
    second_half = 0.5 * second_solved
    upper_term = product(second_half.T, factor_low[0])
    bottom_rows = adjoint_low[0] - 2.0 * (product(second_half, factor_mid) + first_image)
    bottom_solved = right_solve(factor_diag[0], bottom_rows)
    lower_term = product(bottom_solved.T, factor_low[0])
    upper_total = lax.psum(upper_term, ("row", "col"))
    lower_total = lax.psum(lower_term, ("row", "col"))
    top_rows = adjoint_mid - 2.0 * (product(second_grad, factor_mid) + upper_total)
    top_solved = right_solve(factor_diag[0], top_rows)
    first_adjoint = adjoint_diag[0] - product(top_solved.T, factor_mid) - lower_total
    first_grad = diag_adjoint(factor_diag[0], first_adjoint)
    return (
        jnp.stack([first_grad, second_grad]),
        0.5 * top_solved,
        jnp.stack([0.5 * bottom_solved, second_half]),
    )


def solution(mesh):
    return jax.shard_map(
        shards,
        mesh=mesh,
        in_specs=(
            P(),
            P(),
            P(None, ("row", "col"), None),
            P(),
            P(),
            P(None, ("row", "col"), None),
            P("row", None, "col"),
        ),
        out_specs=(P(), P(), P(None, ("row", "col"), None)),
        check_vma=False,
    )
```

profile of v0, /device:TPU:2, one launch (start us, length us, event | category | flops | bytes accessed | tf_op | source)
XLA Modules:
  0.0 587.9 jit_solution(3043104510383694873)
XLA Ops:
  7.2 1.8 fusion.165
  9.8 53.8 %all-gather.5.cloned.1.call-done = f32[1,1024,512]{2,1,0:T(8,128)} async-done(((f32[1,64,512]{2,1,0:T(8,128)}), f32[1,1024,512]{2,1,0:T(8,128)}) %all-gather.5.cloned.1.call-update) | async-done | bytes 2097168 | tf_op jit(solution)/shard_map/all_gather | solution.py:35
  63.6 10.2 %fusion.2 = f32[1024,512]{1,0:T(8,128)} fusion(f32[1024,1024]{0,1:T(8,128)} %bitcast.202, f32[1,1024,512]{2,1,0:T(8,128)} %all-gather.5.cloned.1.call-done), kind=kOutput, calls=%fused_computation.9 | convolution fusion | flops 6442450944 | bytes 8388608 | tf_op jit(solution)/shard_map/dot_general | solution.py:12
  73.8 1.5 copy-done.1
  75.3 1.6 bitcast_select_fusion.1
  76.9 39.0 %all-gather.7.cloned.1.call-done = f32[1,1024,512]{2,1,0:T(8,128)} async-done(((f32[1,64,512]{2,1,0:T(8,128)}), f32[1,1024,512]{2,1,0:T(8,128)}) %all-gather.7.cloned.1.call-update) | async-done | bytes 2097168 | tf_op jit(solution)/shard_map/all_gather | solution.py:35
  115.9 10.2 %fusion = f32[1024,512]{1,0:T(8,128)} fusion(f32[1024,1024]{0,1:T(8,128)} %bitcast.203, f32[1,1024,512]{2,1,0:T(8,128)} %all-gather.7.cloned.1.call-done), kind=kOutput, calls=%fused_computation.7 | convolution fusion | flops 6442450944 | bytes 8388608 | tf_op jit(solution)/shard_map/dot_general | solution.py:12
  126.7 12.0 %while.14 = (s32[]{:T(128)}, f32[512,512]{1,0:T(8,128)}, s32[4,2]{0,1:T(2,128)S(1)}, f32[4,128,128]{2,1,0:T(8,128)S(1)}, s32[]{:T(128)}) while((s32[]{:T(128)}, f32[512,512]{1,0:T(8,128)}, s32[4,2]{0,1:T(2,128)S(1)}, f32[4,128,128]{2,1,0:T(8,128)S(1)}, s32[]{:T(128)}) %tuple.62), condition=%wide.while_cond.1.clone, body=%wide.while_body.1.clone.sunk | while | flops 2 | bytes 131181 | solution.py:18
  127.4 2.3 bitcast_dynamic-update-slice_fusion.4
  130.4 2.3 bitcast_dynamic-update-slice_fusion.4
  133.4 2.3 bitcast_dynamic-update-slice_fusion.4
  136.5 2.3 bitcast_dynamic-update-slice_fusion.4
  138.8 39.3 %custom-call.17 = f32[4,128,128]{1,2,0:T(8,128)S(1)} custom-call(f32[4,128,128]{2,1,0:T(8,128)S(1)} %get-tuple-element.53), custom_call_target="InvertDiagBlocksLowerTriangular" | custom-call | tf_op jit(solution)/shard_map/jit(_solve_triangular)/triangular_solve | solution.py:18
  178.1 7.7 %while.15 = (s32[]{:T(128)}, f32[512,512]{1,0:T(8,128)S(1)}, s32[4,2]{0,1:T(2,128)S(1)}, f32[4,128,128]{2,1,0:T(8,128)S(1)}, s32[]{:T(128)}) while((s32[]{:T(128)}, f32[512,512]{1,0:T(8,128)S(1)}, s32[4,2]{0,1:T(2,128)S(1)}, f32[4,128,128]{2,1,0:T(8,128)S(1)}, s32[]{:T(128)}) %tuple.80), condition=%wide.while_cond.1.clone.3, body=%wide.while_body.1.clone.3.sunk | while | flops 2 | bytes 131181 | solution.py:18
  186.5 40.1 %custom-call.21 = f32[4,128,128]{1,2,0:T(8,128)S(1)} custom-call(f32[4,128,128]{2,1,0:T(8,128)} %copy-done.21), custom_call_target="InvertDiagBlocksLowerTriangular" | custom-call | tf_op jit(solution)/shard_map/jit(_solve_triangular)/triangular_solve | solution.py:18
  232.0 2.0 fusion.77
  234.1 2.0 fusion.79
  236.1 4.7 reduce-scatter.5.cloned.1.call-done
  240.8 1.7 fusion.10
  244.2 2.0 fusion.75
  247.0 265.9 %all-reduce.3.cloned.1.call-done = (f32[512,512]{1,0:T(8,128)}, f32[512,512]{1,0:T(8,128)}, f32[512,512]{1,0:T(8,128)}) async-done(((f32[512,512]{1,0:T(8,128)}, f32[512,512]{1,0:T(8,128)}, f32[512,512]{1,0:T(8,128)}), (f32[512,512]{1,0:T(8,128)}, f32[512,512]{1,0:T(8,128)}, f32[512,512]{1,0:T(8,128)})) %all-reduce.3.cloned.1.call-update) | async-done | bytes 3145744 | tf_op jit(solution)/shard_map/psum | solution.py:43
  512.9 3.7 convolution_bitcast_fusion.1
  516.7 4.7 gather_fusion
  534.7 1.6 copy.29
  536.2 3.8 fusion.7
  543.8 2.2 convolution_subtract_fusion.13
  548.2 1.5 fusion.123
  550.8 3.4 fusion.4
  554.2 1.9 convolution_bitcast_fusion
  556.1 4.8 gather_fusion.1
  576.8 2.1 multiply_bitcast_fusion.1
  579.1 1.8 copy.39
  (148 shorter events, 56.1 us)
Async XLA Ops:
  7.2 233.6 %copy-start = (f32[512,512]{1,0:T(8,128)S(1)}, f32[512,512]{1,0:T(8,128)}, u32[]{:S(2)}) copy-start(f32[512,512]{1,0:T(8,128)} %param.12) | copy-start | bytes 3145732
  7.2 56.4 %all-gather.5.cloned.1.call-start = ((), (), s32[]{:S(2)}) async-start(), calls=%async_computation.4 | async-start | bytes 2228224 | tf_op jit(solution)/shard_map/all_gather | solution.py:35
  9.0 106.9 %all-gather.7.cloned.1.call-start = ((), (), s32[]{:S(2)}) async-start(), calls=%async_computation.5 | async-start | bytes 2228224 | tf_op jit(solution)/shard_map/all_gather | solution.py:35
  9.8 216.9 %reduce-scatter.3.cloned.1.call-start = ((), (), s32[]{:S(2)}) async-start(), calls=%async_computation.2 | async-start | bytes 2228224 | tf_op jit(solution)/shard_map/reduce_scatter | solution.py:36
  73.8 1.6 copy-start.1
  73.8 167.0 %reduce-scatter.5.cloned.1.call-start = ((), (), s32[]{:S(2)}) async-start(), calls=%async_computation.3 | async-start | bytes 2228224 | tf_op jit(solution)/shard_map/reduce_scatter | solution.py:36
  126.1 52.0 %copy-start.3 = (f32[512,512]{1,0:T(8,128)S(1)}, f32[512,512]{1,0:T(8,128)}, u32[]{:S(2)}) copy-start(f32[512,512]{1,0:T(8,128)} %get-tuple-element.169) | copy-start | bytes 3145732
  126.1 100.5 %copy-start.20 = (f32[2,64,512]{2,1,0:T(8,128)S(1)}, f32[2,64,512]{2,1,0:T(8,128)}, u32[]{:S(2)}) copy-start(f32[2,64,512]{2,1,0:T(8,128)} %param.16) | copy-start | bytes 786436
  126.1 105.9 %copy-start.19 = (f32[2,64,512]{2,1,0:T(8,128)S(1)}, f32[2,64,512]{2,1,0:T(8,128)}, u32[]{:S(2)}) copy-start(f32[2,64,512]{2,1,0:T(8,128)} %param.13) | copy-start | bytes 786436
  126.2 386.7 %all-reduce.3.cloned.1.call-start = ((), (), s32[]{:S(2)}) async-start(), calls=%async_computation.6 | async-start | bytes 6291456 | tf_op jit(solution)/shard_map/psum | solution.py:43
  178.1 351.2 %copy-start.15 = (f32[4,128,128]{1,2,0:T(8,128)}, f32[4,128,128]{1,2,0:T(8,128)S(1)}, u32[]{:S(2)}) copy-start(f32[4,128,128]{1,2,0:T(8,128)S(1)} %custom-call.17) | copy-start | bytes 786436
  185.8 0.7 copy-start.21
  226.6 19.6 %copy-start.6 = (f32[4,128,128]{1,2,0:T(8,128)}, f32[4,128,128]{1,2,0:T(8,128)S(1)}, u32[]{:S(2)}) copy-start(f32[4,128,128]{1,2,0:T(8,128)S(1)} %custom-call.21) | copy-start | bytes 786436
  521.4 1.2 copy-start.5
  531.3 4.9 copy-start.9
  531.5 1.4 copy-start.11
  531.6 1.3 copy-start.12
  532.9 0.7 copy-start.13
  536.2 3.8 copy-start.7
  541.6 1.4 copy-start.14
  543.1 0.7 copy-start.16
  548.2 2.6 copy-start.18
  550.8 3.4 copy-start.2
  556.1 5.0 copy-start.8
  560.9 1.2 copy-start.4
  573.6 0.7 copy-start.17
  574.3 2.5 copy-start.10
Sparse Core Ops, SparseCore 0:
  11.0 52.5 all-gather.4
  66.6 49.3 all-gather.6
  119.0 60.3 reduce-scatter.2
  181.8 58.9 reduce-scatter.4
  247.0 265.8 all-reduce.2
where the time goes:
time: 595 us; the launch traced here: 588 us
  waiting for transfers between devices  364 us (61%)
  other arithmetic  88.8 us (15%)
  matrix products  72.7 us (12%)
  local copies, waits for them, and re-layouts  46.4 us (8%)
  between operations  15 us (3%)
    psum x1, waiting for transfers between devices, shards(): lax.psum(product(second_solved.T, factor_low[1]), ('row', 'col'))  266 us
    all_gather x2, waiting for transfers between devices, image_of(): columns = lax.all_gather(panel, 'row', axis=0, tiled=True)  92.8 us
    another operation x4, other arithmetic, right_solve(): jax.scipy.linalg.solve_triangular(factor, row_block.T, trans=1, lower=True)  81 us
    dot_general x10, matrix products, product(): jnp.dot(left_side, right_side, precision=lax.Precision.HIGHEST, preferred...  41 us
    another operation x36, local copies, waits for them, and re-layouts, right_solve(): jax.scipy.linalg.solve_triangular(factor, row_block.T, trans=1, lower=True)  24.7 us
    another operation x35, matrix products, right_solve(): jax.scipy.linalg.solve_triangular(factor, row_block.T, trans=1, lower=True)  22.6 us
  transfers between devices with their start and end apart: 5, of which 4 were waited for; matrix products, arithmetic and copies ran while one was open for 22% of the time, Pallas kernels for 0%

commit v1 on v0

v1 whole, which is shorter than its diff:
```python
import functools
import jax
import jax.numpy as jnp
from jax import lax
from jax.experimental import pallas as pl
from jax.experimental.pallas import tpu as pltpu
from jax.sharding import Mesh, PartitionSpec as P

SIZES = {"y": 4, "x": 4, "z": 8, "c": 2}
TILE = 128


F32 = jnp.float32
BF16 = jnp.bfloat16
VMEM = pl.BlockSpec(memory_space=pltpu.VMEM)
SMEM = pl.BlockSpec(memory_space=pltpu.SMEM)
NN, TN = ((1,), (0,)), ((0,), (0,))


def product(left_side, right_side, dims=NN):
    return lax.dot_general(
        left_side, right_side, (dims, ((), ())), precision=lax.Precision.HIGHEST, preferred_element_type=F32
    )


def split(value):
    high = value.astype(BF16)
    return high, (value - high.astype(F32)).astype(BF16)


def pair_product(left_side, right_side, dims=NN):
    one = functools.partial(lax.dot_general, dimension_numbers=(dims, ((), ())), preferred_element_type=F32)
    return (
        one(left_side[0], right_side[0])
        + (one(left_side[0], right_side[1]) + one(left_side[1], right_side[0]))
    )


def call(kernel, outs, flops, grid=None, in_specs=None, out_specs=None, scratch=()):
    specs = {} if grid is None else {"grid": grid}
    return pl.pallas_call(
        kernel,
        out_shape=outs,
        in_specs=in_specs,
        out_specs=out_specs,
        scratch_shapes=scratch,
        cost_estimate=pl.CostEstimate(flops=flops, bytes_accessed=8 * 2**20, transcendentals=0),
        **specs,
    )


def array(*shape):
    return jax.ShapeDtypeStruct(shape, F32)


def matmul(left_side, right_side, dims=NN):
    if dims == TN:
        left_side = left_side.T
    return pair_product(split(left_side), split(right_side))


def invert_kernel(factor, out, blocks, parts):
    count, size = factor.shape[0], factor.shape[1]
    row = lax.broadcasted_iota(jnp.int32, (TILE, TILE), 0)
    column = lax.broadcasted_iota(jnp.int32, (TILE, TILE), 1)
    eye = row == column
    per = size // TILE
    for p in range(count):
        for b in range(per):
            at = slice(b * TILE, (b + 1) * TILE)
            block = factor[p, at, at]
            blocks[p * per + b] = block
            parts[p * per + b] = jnp.where(eye, 1.0 / jnp.where(eye, block, 1.0), 0.0)

    def level(step, carry):
        high, low = lax.shift_right_logical(row, step), lax.shift_right_logical(column, step)
        corner = (high == low + 1) & ((high & 1) == 1)
        slots = range(count * per)
        halves = [product(jnp.where(corner, blocks[s], 0.0), parts[s]) for s in slots]
        news = [parts[s] - product(parts[s], halves[s]) for s in slots]
        for s in slots:
            parts[s] = news[s]
        return carry

    lax.fori_loop(0, TILE.bit_length() - 1, level, 0)
    out[...] = jnp.zeros_like(out)
    for p in range(count):
        for b in range(per):
            at = slice(b * TILE, (b + 1) * TILE)
            out[p, at, at] = parts[p * per + b]
    step = TILE
    while step < size:
        for p in range(count):
            for start in range(0, size, 2 * step):
                low, mid, high = start, start + step, start + 2 * step
                half = product(factor[p, mid:high, low:mid], out[p, low:mid, low:mid])
                out[p, mid:high, low:mid] = -product(out[p, mid:high, mid:high], half)
        step *= 2


def invert(factor_diag):
    count, size = factor_diag.shape[0], factor_diag.shape[1]
    blocks = pltpu.VMEM((count * size // TILE, TILE, TILE), F32)
    return call(
        invert_kernel, array(*factor_diag.shape), 10**10,
        in_specs=[VMEM], out_specs=VMEM, scratch=[blocks, blocks],
    )(factor_diag)


def constants_kernel(factor, mid, adjoint, adjoint_mid, inverses, solved, second, first):
    solved[...] = matmul(inverses[1], mid[...])
    second[...] = matmul(factor[1], adjoint[1], TN)
    first[...] = matmul(factor[0], adjoint[0], TN) - matmul(adjoint_mid[...], mid[...], TN)


def constants(factor_diag, factor_mid, adjoint_diag, adjoint_mid, inverses):
    square = array(*factor_mid.shape)
    return call(
        constants_kernel, (square, square, square), 5 * 10**9,
        in_specs=[VMEM] * 5, out_specs=(VMEM,) * 3,
    )(factor_diag, factor_mid, adjoint_diag, adjoint_mid, inverses)


def turn_kernel(block, high, low):
    high[...], low[...] = split(block[...].T)


def turn(flipped):
    count, depth = flipped.shape
    step = min(256, depth)
    out = jax.ShapeDtypeStruct((depth, count), BF16)
    tall = pl.BlockSpec((step, count), lambda i: (i, 0))
    return call(
        turn_kernel, (out, out), 10**9,
        grid=(depth // step,),
        in_specs=[pl.BlockSpec((count, step), lambda i: (0, i))],
        out_specs=(tall, tall),
    )(flipped)


def first_image_kernel(offsets, place, block, near, near_other, far, far_other, out, high, low):
    chip, core = place[0], place[1]
    rows = near.shape[1]

    @pl.when(pl.program_id(0) == 0)
    def _():
        index = 0
        for mine, other in ((near, near_other), (far, far_other)):
            for slot in range(mine.shape[0]):
                at = lax.rem(chip + offsets[index] + SIZES["z"], SIZES["z"]) * 2
                for ref, owner in ((mine, core), (other, 1 - core)):
                    where = pl.ds(pl.multiple_of((at + owner) * rows, rows), rows)
                    high[where, :], low[where, :] = split(ref[slot])
                index += 1

    out[...] = pair_product(split(block[...]), (high[...], low[...]))


def first_image(offsets, place, flipped, near, near_other, far, far_other):
    count, depth = flipped.shape
    size = near.shape[2]
    step = min(512, count)
    whole = lambda v: pl.BlockSpec(v.shape, lambda i: (0, 0, 0), pipeline_mode=pl.Buffered(1))
    gathered = (near, near_other, far, far_other)
    return call(
        functools.partial(first_image_kernel, offsets), array(count, size), 3 * 10**9,
        grid=(count // step,),
        in_specs=[SMEM, pl.BlockSpec((step, depth), lambda i: (i, 0))] + [whole(v) for v in gathered],
        out_specs=pl.BlockSpec((step, size), lambda i: (i, 0)),
        scratch=[pltpu.VMEM((depth, size), BF16)] * 2,
    )(place, flipped, *gathered)


def second_image_kernel(place, high, low, columns, keep, give, right_high, right_low):
    chip, core = place[0], place[1]
    rows = keep.shape[1]

    @pl.when(pl.program_id(0) == 0)
    def _():
        right_high[...], right_low[...] = split(columns[...])

    value = pair_product((high[...], low[...]), (right_high[...], right_low[...]))
    chips = value.shape[0] // (2 * rows)
    for n in range(chips):
        slot = lax.rem(pl.program_id(0) * chips + n - chip + SIZES["z"], SIZES["z"])
        even = value[2 * n * rows : (2 * n + 1) * rows, :]
        odd = value[(2 * n + 1) * rows : (2 * n + 2) * rows, :]
        keep[slot] = jnp.where(core == 0, even, odd)
        give[slot] = jnp.where(core == 0, odd, even)


def second_image(place, high, low, columns):
    depth, count = high.shape
    size = columns.shape[1]
    step = min(512, depth)
    tall = pl.BlockSpec((step, count), lambda i: (i, 0))
    rows = depth // (2 * SIZES["z"])
    out = array(SIZES["z"], rows, size)
    spec = pl.BlockSpec(out.shape, lambda i: (0, 0, 0))
    return call(
        second_image_kernel, (out, out), 3 * 10**9,
        grid=(depth // step,),
        in_specs=[
            SMEM, tall, tall, pl.BlockSpec((count, size), lambda i: (0, 0), pipeline_mode=pl.Buffered(1)),
        ],
        out_specs=(spec, spec),
        scratch=[pltpu.VMEM((count, size), BF16)] * 2,
    )(place, high, low, columns)


def terms_kernel(place, second_sum, pieces, adjoint, factor, keep, give, rows, second_second, second_first, first_first):
    size = second_sum.shape[1]
    per = size // TILE
    middle = size // 2
    first_sum = pieces[0]
    for n in range(1, pieces.shape[0]):
        first_sum = first_sum + pieces[n]
    second = adjoint[1] - 2.0 * second_sum[...]
    first = adjoint[0] - 2.0 * first_sum
    rows[1], rows[0] = second, first

    def put(ref, at, cols, left, right):
        ref[at, cols] = pair_product(tuple(v[at, :] for v in left), tuple(v[:, cols] for v in right))

    second, first = split(second.T), split(first.T)
    second_right, first_right = split(factor[1]), split(factor[0])
    top, low, full = slice(0, middle), slice(middle, size), slice(0, size)
    put(second_first, full, full, second, first_right)
    put(second_second, top, top, second, second_right)
    put(second_second, low, full, second, second_right)
    put(first_first, top, top, first, first_right)
    put(first_first, low, full, first, first_right)

    lower = [(i, j) for i in range(per) for j in range(i + 1)]
    square = [(i, j) for i in range(per) for j in range(per)]
    tiles = [(second_second, at) for at in lower] + [(second_first, at) for at in square]
    tiles += [(first_first, at) for at in lower]
    half = len(tiles) // 2

    def store(out, chosen):
        for n, (ref, (i, j)) in enumerate(chosen):
            out[n * TILE : (n + 1) * TILE, :] = ref[
                i * TILE : (i + 1) * TILE, j * TILE : (j + 1) * TILE
            ]

    @pl.when(place[1] == 0)
    def _():
        store(keep, tiles[:half])
        store(give, tiles[half:])

    @pl.when(place[1] == 1)
    def _():
        store(keep, tiles[half:])
        store(give, tiles[:half])


def terms(place, second_sum, pieces, adjoint_low, factor_low):
    size = second_sum.shape[1]
    per = size // TILE
    half = per * (2 * per + 1) // 2 * TILE
    return call(
        terms_kernel, (array(half, TILE), array(half, TILE), array(*adjoint_low.shape)), 10**9,
        in_specs=[SMEM] + [VMEM] * 4,
        out_specs=(VMEM,) * 3,
        scratch=[pltpu.VMEM((size, size), F32)] * 3,
    )(place, second_sum, pieces, adjoint_low, factor_low)


def rows_kernel(rows, inverses, solved, out):
    out[1] = 0.5 * matmul(rows[1], inverses[1])
    out[0] = 0.5 * matmul(rows[0] - matmul(rows[1], solved[...]), inverses[0])


def finish_kernel(
    place, mine, other, inverses, solved, second_const, first_const, adjoint_mid, diag, top, second, cross, first
):
    size = solved.shape[0]
    core = place[1]
    per = size // TILE
    half = mine.shape[0] // TILE
    upper = lax.broadcasted_iota(jnp.int32, (TILE, TILE), 0) < lax.broadcasted_iota(
        jnp.int32, (TILE, TILE), 1
    )

    def tile(index):
        part, row = divmod(index, half)
        rows = slice(row * TILE, (row + 1) * TILE)
        return jnp.where(core == part, mine[rows, :], other[rows, :])

    def at(i, j):
        return (slice(i * TILE, (i + 1) * TILE), slice(j * TILE, (j + 1) * TILE))

    def mirror(value, ref):
        for i in range(per):
            for j in range(i + 1):
                part = value(i, j)
                if i == j:
                    ref[at(i, j)] = jnp.where(upper, part.T, part)
                else:
                    ref[at(i, j)] = part
                    ref[at(j, i)] = part.T

    low = per * (per + 1) // 2
    number = lambda i, j: i * (i + 1) // 2 + j
    mirror(lambda i, j: second_const[at(i, j)] - tile(number(i, j)), second)
    for i in range(per):
        for j in range(per):
            cross[at(i, j)] = tile(low + i * per + j)
    known = solved[...]
    image = matmul(second[...], known)
    outer = matmul(known, 0.5 * image + cross[...], TN)
    outer = outer + outer.T

    def first_value(i, j):
        return first_const[at(i, j)] - tile(low + per * per + number(i, j)) + outer[at(i, j)]

    mirror(first_value, first)
    diag[0] = 0.5 * matmul(matmul(inverses[0], first[...], TN), inverses[0])
    diag[1] = 0.5 * matmul(matmul(inverses[1], second[...], TN), inverses[1])
    rest = adjoint_mid[...] - matmul(inverses[1], image + cross[...], TN)
    top[...] = 0.5 * matmul(rest, inverses[0])


def finish(place, tiles, other, inverses, mid_solved, second_const, first_const, adjoint_mid):
    size = mid_solved.shape[0]
    return call(
        finish_kernel, (array(2, size, size), array(size, size)), 10**10,
        in_specs=[SMEM] + [VMEM] * 7, out_specs=(VMEM, VMEM),
        scratch=[pltpu.VMEM((size, size), F32)] * 3,
    )(place, tiles, other, inverses, mid_solved, second_const, first_const, adjoint_mid)


def shift(value, axis, step):
    size = SIZES[axis]
    return lax.ppermute(value, axis, [(i, (i + step) % size) for i in range(size)])


def ring_sum(blocks, axis):
    size = SIZES[axis]
    far = blocks[size // 2]
    half = far.shape[0] // 2
    ahead, behind = shift(far[:half], axis, 1), shift(far[half:], axis, -1)
    for step in range(size // 2 - 1, 0, -1):
        up, down = blocks[step], blocks[size - step]
        if step == size // 2 - 1:
            up = jnp.concatenate([up[:half] + ahead, up[half:]])
            down = jnp.concatenate([down[:half], down[half:] + behind])
        else:
            up, down = up + ahead, down + behind
        ahead, behind = shift(up, axis, 1), shift(down, axis, -1)
    return blocks[0] + ahead + behind


def spread(value, axes, parts):
    return lax.all_to_all(jnp.broadcast_to(value[None], (parts,) + value.shape), axes, 0, 0)


def shards(
    factor_diag, factor_mid, factor_low, adjoint_diag, adjoint_mid, adjoint_low, trailing_adjoint
):
    size = factor_mid.shape[0]
    rows = factor_low.shape[1]
    block_rows, row_groups, group_cols = trailing_adjoint.shape
    flipped = trailing_adjoint.transpose(1, 2, 0).reshape(row_groups * group_cols, block_rows)
    place = jnp.stack([lax.axis_index("z"), lax.axis_index("c")]).astype(jnp.int32)
    parts = SIZES["y"] * SIZES["x"]

    columns = spread(factor_low[1], ("y", "x"), parts).reshape(-1, size)

    own, half = factor_low[0], rows // 2
    ahead, behind = [own], [own]
    for _ in range(1, 4):
        ahead.append(shift(ahead[-1], "z", 1))
        behind.append(shift(behind[-1], "z", -1))
    across = jnp.concatenate([shift(ahead[3][:half], "z", 1), shift(behind[3][half:], "z", -1)])
    near = jnp.stack([own, ahead[1], behind[1], ahead[2], behind[2]])
    far = jnp.stack([ahead[3], behind[3], across])
    high, low = turn(flipped)
    images = first_image(
        (0, -1, 1, -2, 2, -3, 3, 4), place, flipped, near, shift(near, "c", 1), far, shift(far, "c", 1)
    )
    pieces = lax.all_to_all(images.reshape(parts, rows, size), ("y", "x"), 0, 0)
    keep, give = second_image(place, high, low, columns)
    second_sum = ring_sum(keep + shift(give, "c", 1), "z")

    keep, give, sides = terms(place, second_sum, pieces, adjoint_low, factor_low)
    keep = keep + shift(give, "c", 1)
    tiles = lax.all_to_all(keep.reshape(parts, -1, TILE), ("y", "x"), 0, 0)
    tiles = spread(tiles.sum(0), "z", SIZES["z"])
    tiles = spread(tiles.sum(0), ("y", "x"), parts).reshape(-1, TILE)
    other = shift(tiles, "c", 1)
    inverses = invert(factor_diag)
    mid_solved, second_const, first_const = constants(
        factor_diag, factor_mid, adjoint_diag, adjoint_mid, inverses
    )
    low = call(
        rows_kernel, array(2, rows, size), 10**9, in_specs=[VMEM] * 3, out_specs=VMEM
    )(sides, inverses, mid_solved)
    diag, top = finish(place, tiles, other, inverses, mid_solved, second_const, first_const, adjoint_mid)
    return diag, top, low


def solution(mesh):
    axes = tuple(SIZES)
    torus = Mesh(mesh.devices.reshape(tuple(SIZES.values())), axes)
    low = P(None, axes, None)

    return jax.shard_map(
        shards,
        mesh=torus,
        in_specs=(P(), P(), low, P(), P(), low, P(("y", "x"), None, ("z", "c"))),
        out_specs=(P(), P(), low),
        check_vma=False,
    )
```

time: 595 us -> 222 us (0.37)
  waiting for transfers between devices: 364 us -> 30.7 us
  other arithmetic: 88.8 us -> 4.36 us
  matrix products: 72.7 us -> 0 us
  blocking collectives: 0 us -> 68.8 us
  Pallas kernels: 0 us -> 61 us
  starting transfers between devices: 0.67 us -> 45.3 us
  local copies, waits for them, and re-layouts: 46.4 us -> 8.07 us
  between operations: 15 us -> 0.85 us
    psum x1 -> x0, waiting for transfers between devices: 266 us -> none  [shards(): lax.psum(product(second_solved.T, factor_low[1]), ('row', 'col'))]
    all_gather x2 -> x0, waiting for transfers between devices: 92.8 us -> none  [image_of(): columns = lax.all_gather(panel, 'row', axis=0, tiled=True)]
    another operation x8 -> x3, other arithmetic: 84 us -> 0.62 us  [the longest x1 0.59 us: shards(): jnp.stack([lax.axis_index('z'), lax.axis_index('c')]).astype(jnp.int32)]
    all_to_all x0 -> x3, blocking collectives: none -> 68.8 us  [the longest x2 44 us: spread(): lax.all_to_all(jnp.broadcast_to(value[None], (parts,) + value.shape), axe...]
    pallas_call x0 -> x8, Pallas kernels: none -> 61 us  [the longest x1 13.1 us: invert(): call(invert_kernel, array(*factor_diag.shape), 10 ** 10, in_specs=[VMEM],...]
    dot_general x10 -> x0, matrix products: 41 us -> none  [product(): jnp.dot(left_side, right_side, precision=lax.Precision.HIGHEST, preferred...]
    another operation x49 -> x0, matrix products: 31.7 us -> none  [the longest x35 22.6 us: right_solve(): jax.scipy.linalg.solve_triangular(factor, row_block.T, trans=1, lower=True)]
    ppermute x0 -> x21, waiting for transfers between devices: none -> 30.7 us  [shift(): lax.ppermute(value, axis, [(i, (i + step) % size) for i in range(size)])]
  transfers between devices with their start and end apart: 5 -> 23, of which waited for: 4 -> 9; matrix products, arithmetic and copies ran while one was open for 22% -> 1% of each run, Pallas kernels for 0% -> 20%
where the time goes in v1:
time: 222 us; the launch traced here: 219 us
  blocking collectives  68.8 us (31%)
  Pallas kernels  61 us (27%)
  starting transfers between devices  45.3 us (20%)
  waiting for transfers between devices  30.7 us (14%)
  local copies, waits for them, and re-layouts  8.07 us (4%)
  other arithmetic  4.36 us (2%)
    all_to_all x2, blocking collectives, spread(): lax.all_to_all(jnp.broadcast_to(value[None], (parts,) + value.shape), axe...  44 us
    ppermute x21, waiting for transfers between devices, shift(): lax.ppermute(value, axis, [(i, (i + step) % size) for i in range(size)])  30.7 us
    ppermute x21, starting transfers between devices, shift(): lax.ppermute(value, axis, [(i, (i + step) % size) for i in range(size)])  29.8 us
    all_to_all x1, blocking collectives, shards(): tiles = lax.all_to_all(keep.reshape(parts, -1, TILE), ('y', 'x'), 0, 0)  24.7 us
    pallas_call x1, Pallas kernels, invert(): call(invert_kernel, array(*factor_diag.shape), 10 ** 10, in_specs=[VMEM],...  13.1 us
    pallas_call x1, Pallas kernels, finish(): call(finish_kernel, (array(2, size, size), array(size, size)), 10 ** 10,...  11.8 us
    all_to_all x1, starting transfers between devices, shards(): pieces = lax.all_to_all(images.reshape(parts, rows, size), ('y', 'x'), 0, 0)  7.98 us
    pallas_call x1, Pallas kernels, constants(): call(constants_kernel, (square, square, square), 5 * 10 ** 9, in_specs=[V...  7.88 us
  transfers between devices with their start and end apart: 23, of which 9 were waited for; matrix products, arithmetic and copies ran while one was open for 1% of the time, Pallas kernels for 20%

profile of v1, /device:TPU:2, one launch (start us, length us, event | category | flops | bytes accessed | tf_op | source)
XLA Modules:
  0.0 219.0 jit_solution(5943809213976720873)
XLA Ops:
  1.6 1.6 broadcast_in_dim.9
  3.2 7.5 %all-to-all-start = ((f32[16,64,512]{2,1,0:T(8,128)}), f32[16,64,512]{2,1,0:T(8,128)S(1)}, u32[]{:S(2)}, u32[]{:S(2)}) async-start(f32[16,64,512]{2,1,0:T(8,128)} %broadcast_in_dim.9), calls=%async_computation | async-start | bytes 4194304 | tf_op jit(solution)/shard_map/all_to_all | solution.py:355
  10.7 1.9 collective-permute-start.9
  12.6 4.0 %collective-permute-start.10 = (f32[64,512]{1,0:T(8,128)S(1)}, f32[64,512]{1,0:T(8,128)S(1)}, u32[]{:S(2)}, u32[]{:S(2)}) collective-permute-start(f32[64,512]{1,0:T(8,128)S(1)} %get-tuple-element.35), channel_id=1, source_target_pairs={{0,14},{2,0},{4,2},{6,4},{8,6},{10,8},{12,10},{14,12},{1,15},{3,1}... | collective-permute-start | bytes 393224 | tf_op jit(solution)/shard_map/ppermute | solution.py:335
  16.7 5.3 %shard_map.94 = (bf16[1024,1024]{1,0:T(8,128)(2,1)}, bf16[1024,1024]{1,0:T(8,128)(2,1)}) custom-call(f32[1024,1024]{1,0:T(8,128)} %bitcast.64), custom_call_target="tpu_custom_call" | custom-call | flops 1000000000 | bytes 8388608 | tf_op jit(solution)/shard_map/pallas_call | solution.py:133
  22.6 3.2 %collective-permute-start.12 = (f32[64,512]{1,0:T(8,128)S(1)}, f32[64,512]{1,0:T(8,128)S(1)}, u32[]{:S(2)}, u32[]{:S(2)}) collective-permute-start(f32[64,512]{1,0:T(8,128)S(1)} %collective-permute-done.10), channel_id=1, source_target_pairs={{0,14},{2,0},{4,2},{6,4},{8,6},{10,8},{12,10},{14,12},{1,15},{3,1}... | collective-permute-start | bytes 393224 | tf_op jit(solution)/shard_map/ppermute | solution.py:335
  25.8 2.9 %collective-permute-done.11 = f32[64,512]{1,0:T(8,128)S(1)} collective-permute-done((f32[64,512]{1,0:T(8,128)S(1)}, f32[64,512]{1,0:T(8,128)S(1)}, u32[]{:S(2)}, u32[]{:S(2)}) %collective-permute-start.11) | collective-permute-done | bytes 131104 | tf_op jit(solution)/shard_map/ppermute | solution.py:335
  28.7 3.2 %collective-permute-start.15 = (f32[64,512]{1,0:T(8,128)S(1)}, f32[64,512]{1,0:T(8,128)S(1)}, u32[]{:S(2)}, u32[]{:S(2)}) collective-permute-start(f32[64,512]{1,0:T(8,128)S(1)} %collective-permute-done.12), channel_id=1, source_target_pairs={{0,14},{2,0},{4,2},{6,4},{8,6},{10,8},{12,10},{14,12},{1,15},{3,1}... | collective-permute-start | bytes 393224 | tf_op jit(solution)/shard_map/ppermute | solution.py:335
  32.0 2.9 %collective-permute-done.14 = f32[64,512]{1,0:T(8,128)S(1)} collective-permute-done((f32[64,512]{1,0:T(8,128)S(1)}, f32[64,512]{1,0:T(8,128)S(1)}, u32[]{:S(2)}, u32[]{:S(2)}) %collective-permute-start.14) | collective-permute-done | bytes 131104 | tf_op jit(solution)/shard_map/ppermute | solution.py:335
  35.0 3.3 %collective-permute-start.17 = (f32[32,512]{1,0:T(8,128)S(1)}, f32[32,512]{1,0:T(8,128)S(1)}, u32[]{:S(2)}, u32[]{:S(2)}) collective-permute-start(f32[32,512]{1,0:T(8,128)S(1)} %slice.105), channel_id=1, source_target_pairs={{0,14},{2,0},{4,2},{6,4},{8,6},{10,8},{12,10},{14,12},{1,15},{3,1}... | collective-permute-start | bytes 196616 | tf_op jit(solution)/shard_map/ppermute | solution.py:335
  39.6 7.5 %shard_map.95 = (f32[8,64,512]{2,1,0:T(8,128)}, f32[8,64,512]{2,1,0:T(8,128)}) custom-call(s32[2]{0:T(128)} %pad_add_fusion.place, bf16[1024,1024]{1,0:T(8,128)(2,1)} %get-tuple-element.15.high, bf16[1024,1024]{1,0:T(8,128)(2,1)} %get-tuple-element.16.low, f32[1024,512]{1,0:T(8,128)} %bitcast.67), custom_call_target="tpu_custom_call" | custom-call | flops 3000000000 | bytes 8388608 | tf_op jit(solution)/shard_map/pallas_call | solution.py:200
  47.9 3.6 %collective-permute-done.18.far_other = f32[3,64,512]{2,1,0:T(8,128)S(1)} collective-permute-done((f32[3,64,512]{2,1,0:T(8,128)S(1)}, f32[3,64,512]{2,1,0:T(8,128)S(1)}, u32[]{:S(2)}, u32[]{:S(2)}) %collective-permute-start.18) | collective-permute-done | bytes 393248 | tf_op jit(solution)/shard_map/ppermute | solution.py:335
  53.1 7.0 %shard_map.96 = f32[1024,512]{1,0:T(8,128)} custom-call(s32[2]{0:T(128)} %pad_add_fusion.place, f32[1024,1024]{1,0:T(8,128)} %bitcast.65, f32[5,64,512]{2,1,0:T(8,128)} %copy-done.5, f32[5,64,512]{2,1,0:T(8,128)} %copy-done.7, f32[3,64,512]{2,1,0:T(8,128)} %copy-done.4, f32[3,64,512]{2,1,0:T(8,128)} %copy-done.8), custom_call_target="tpu_custom_call" | custom-call | flops 3000000000 | bytes 8388608 | tf_op jit(solution)/shard_map/pallas_call | solution.py:165
  60.1 8.0 %all-to-all-start.1 = ((f32[16,64,512]{2,1,0:T(8,128)}), f32[16,64,512]{2,1,0:T(8,128)S(1)}, u32[]{:S(2)}, u32[]{:S(2)}) async-start(f32[16,64,512]{2,1,0:T(8,128)} %bitcast.66), calls=%async_computation.1 | async-start | bytes 4194304 | tf_op jit(solution)/shard_map/all_to_all | solution.py:382
  69.5 2.2 collective-permute-start.1
  71.7 4.0 %collective-permute-start.5 = (f32[32,512]{1,0:T(8,128)S(1)}, f32[32,512]{1,0:T(8,128)S(1)}, u32[]{:S(2)}, u32[]{:S(2)}) collective-permute-start(f32[32,512]{1,0:T(8,128)S(1)} %get-tuple-element.32), channel_id=1, source_target_pairs={{0,14},{2,0},{4,2},{6,4},{8,6},{10,8},{12,10},{14,12},{1,15},{3,1}... | collective-permute-start | bytes 196616 | tf_op jit(solution)/shard_map/ppermute | solution.py:335
  75.7 2.2 collective-permute-done.1
  78.1 3.4 %collective-permute-start.6 = (f32[64,512]{1,0:T(8,128)S(1)}, f32[64,512]{1,0:T(8,128)S(1)}, u32[]{:S(2)}, u32[]{:S(2)}) collective-permute-start(f32[64,512]{1,0:T(8,128)S(1)} %pad_maximum_fusion.2), channel_id=1, source_target_pairs={{0,14},{2,0},{4,2},{6,4},{8,6},{10,8},{12,10},{14,12},{1,15},{3,1}... | collective-permute-start | bytes 393224 | tf_op jit(solution)/shard_map/ppermute | solution.py:335
  81.4 2.8 %collective-permute-done.2 = f32[64,512]{1,0:T(8,128)S(1)} collective-permute-done((f32[64,512]{1,0:T(8,128)S(1)}, f32[64,512]{1,0:T(8,128)S(1)}, u32[]{:S(2)}, u32[]{:S(2)}) %collective-permute-start.2) | collective-permute-done | bytes 131104 | tf_op jit(solution)/shard_map/ppermute | solution.py:335
  84.4 6.2 %collective-permute-done.3 = f32[64,512]{1,0:T(8,128)S(1)} collective-permute-done((f32[64,512]{1,0:T(8,128)S(1)}, f32[64,512]{1,0:T(8,128)S(1)}, u32[]{:S(2)}, u32[]{:S(2)}) %collective-permute-start.3) | collective-permute-done | bytes 131104 | tf_op jit(solution)/shard_map/ppermute | solution.py:335
  92.7 3.5 %collective-permute-done.7 = f32[64,512]{1,0:T(8,128)S(1)} collective-permute-done((f32[64,512]{1,0:T(8,128)S(1)}, f32[64,512]{1,0:T(8,128)S(1)}, u32[]{:S(2)}, u32[]{:S(2)}) %collective-permute-start.7) | collective-permute-done | bytes 131104 | tf_op jit(solution)/shard_map/ppermute | solution.py:335
  96.3 1.5 collective-permute-start.8
  97.8 3.5 %collective-permute-done.8 = f32[64,512]{1,0:T(8,128)S(1)} collective-permute-done((f32[64,512]{1,0:T(8,128)S(1)}, f32[64,512]{1,0:T(8,128)S(1)}, u32[]{:S(2)}, u32[]{:S(2)}) %collective-permute-start.8) | collective-permute-done | bytes 131104 | tf_op jit(solution)/shard_map/ppermute | solution.py:335
  103.3 4.7 %shard_map.97 = (f32[2304,128]{1,0:T(8,128)}, f32[2304,128]{1,0:T(8,128)}, f32[2,64,512]{2,1,0:T(8,128)}) custom-call(s32[2]{0:T(128)} %pad_add_fusion.place, f32[64,512]{1,0:T(8,128)} %fusion.5.second_sum, f32[16,64,512]{2,1,0:T(8,128)} %copy-done, f32[2,64,512]{2,1,0:T(8,128)} %adjoint.2, f32[2,64,512]{2,1,0:T(8,128)} %factor.3), custom_call_target="tpu_custom_call" | custom-call | flops 1000000000 | bytes 8388608 | tf_op jit(solution)/shard_map/pallas_call | solution.py:261
  108.0 3.1 %collective-permute-done.19 = f32[2304,128]{1,0:T(8,128)S(1)} collective-permute-done((f32[2304,128]{1,0:T(8,128)}, f32[2304,128]{1,0:T(8,128)S(1)}, u32[]{:S(2)}, u32[]{:S(2)}) %collective-permute-start.19) | collective-permute-done | bytes 1179680 | tf_op jit(solution)/shard_map/ppermute | solution.py:335
  112.5 24.7 %all_to_all.25 = f32[16,144,128]{2,1,0:T(8,128)S(1)} all-to-all(f32[16,144,128]{2,1,0:T(8,128)S(1)} %bitcast.63), channel_id=1, replica_groups=mesh['y'=4,'x'=4,'z'=8,'c'=2] {'y','x'}, dimensions={0} | all-to-all | bytes 2359296 | tf_op jit(solution)/shard_map/all_to_all | solution.py:388
  137.3 23.7 %all_to_all.26 = f32[8,144,128]{2,1,0:T(8,128)S(1)} all-to-all(f32[8,144,128]{2,1,0:T(8,128)S(1)} %broadcast_in_dim.10), channel_id=1, replica_groups=mesh['y'=4,'x'=4,'z'=8,'c'=2] {'z'}, dimensions={0} | all-to-all | bytes 1179648 | tf_op jit(solution)/shard_map/all_to_all | solution.py:355
  161.1 20.4 %all_to_all.27 = f32[16,144,128]{2,1,0:T(8,128)S(1)} all-to-all(f32[16,144,128]{2,1,0:T(8,128)S(1)} %broadcast_in_dim.22), channel_id=1, replica_groups=mesh['y'=4,'x'=4,'z'=8,'c'=2] {'y','x'}, dimensions={0} | all-to-all | bytes 2359296 | tf_op jit(solution)/shard_map/all_to_all | solution.py:355
  181.5 13.1 %shard_map.98.inverses = f32[2,512,512]{2,1,0:T(8,128)} custom-call(f32[2,512,512]{2,1,0:T(8,128)} %factor.5), custom_call_target="tpu_custom_call" | custom-call | flops 10000000000 | bytes 8388608 | tf_op jit(solution)/shard_map/pallas_call | solution.py:104
  194.6 7.9 %shard_map.99 = (f32[512,512]{1,0:T(8,128)}, f32[512,512]{1,0:T(8,128)}, f32[512,512]{1,0:T(8,128)}) custom-call(f32[2,512,512]{2,1,0:T(8,128)} %factor.5, f32[512,512]{1,0:T(8,128)} %mid.1, f32[2,512,512]{2,1,0:T(8,128)} %adjoint.3, f32[512,512]{1,0:T(8,128)} %adjoint_mid.3, f32[2,512,512]{2,1,0:T(8,128)} %shard_map.98.inverses), custom_call_target="tpu_custom_call" | custom-call | flops 5000000000 | bytes 8388608 | tf_op jit(solution)/shard_map/pallas_call | solution.py:118
  202.5 3.7 %shard_map.101 = f32[2,64,512]{2,1,0:T(8,128)} custom-call(f32[2,64,512]{2,1,0:T(8,128)} %get-tuple-element.26.rows, f32[2,512,512]{2,1,0:T(8,128)} %shard_map.98.inverses, f32[512,512]{1,0:T(8,128)} %get-tuple-element.21.solved), custom_call_target="tpu_custom_call" | custom-call | flops 1000000000 | bytes 8388608 | tf_op jit(solution)/shard_map/pallas_call | solution.py:396
  207.2 11.8 %shard_map.100 = (f32[2,512,512]{2,1,0:T(8,128)}, f32[512,512]{1,0:T(8,128)}) custom-call(s32[2]{0:T(128)} %pad_add_fusion.place, f32[2304,128]{1,0:T(8,128)} %bitcast.69, f32[2304,128]{1,0:T(8,128)} %copy-done.6, f32[2,512,512]{2,1,0:T(8,128)} %shard_map.98.inverses, f32[512,512]{1,0:T(8,128)} %get-tuple-element.21.solved, ...), custom_call_target="tpu_custom_call" | custom-call | flops 10000000000 | bytes 8388608 | tf_op jit(solution)/shard_map/pallas_call | solution.py:326
  (68 shorter events, 13.9 us)
Async XLA Ops:
  3.2 35.0 %all-to-all-start = ((f32[16,64,512]{2,1,0:T(8,128)}), f32[16,64,512]{2,1,0:T(8,128)S(1)}, u32[]{:S(2)}, u32[]{:S(2)}) async-start(f32[16,64,512]{2,1,0:T(8,128)} %broadcast_in_dim.9), calls=%async_computation | async-start | bytes 4194304 | tf_op jit(solution)/shard_map/all_to_all | solution.py:355
  10.7 11.8 %collective-permute-start.9 = (f32[64,512]{1,0:T(8,128)S(1)}, f32[64,512]{1,0:T(8,128)S(1)}, u32[]{:S(2)}, u32[]{:S(2)}) collective-permute-start(f32[64,512]{1,0:T(8,128)S(1)} %get-tuple-element.35), channel_id=1, source_target_pairs={{0,2},{2,4},{4,6},{6,8},{8,10},{10,12},{12,14},{14,0},{1,3},{3,5},... | collective-permute-start | bytes 393224 | tf_op jit(solution)/shard_map/ppermute | solution.py:335
  12.6 9.9 %collective-permute-start.10 = (f32[64,512]{1,0:T(8,128)S(1)}, f32[64,512]{1,0:T(8,128)S(1)}, u32[]{:S(2)}, u32[]{:S(2)}) collective-permute-start(f32[64,512]{1,0:T(8,128)S(1)} %get-tuple-element.35), channel_id=1, source_target_pairs={{0,14},{2,0},{4,2},{6,4},{8,6},{10,8},{12,10},{14,12},{1,15},{3,1}... | collective-permute-start | bytes 393224 | tf_op jit(solution)/shard_map/ppermute | solution.py:335
  22.6 6.2 %collective-permute-start.11 = (f32[64,512]{1,0:T(8,128)S(1)}, f32[64,512]{1,0:T(8,128)S(1)}, u32[]{:S(2)}, u32[]{:S(2)}) collective-permute-start(f32[64,512]{1,0:T(8,128)S(1)} %collective-permute-done.9), channel_id=1, source_target_pairs={{0,2},{2,4},{4,6},{6,8},{8,10},{10,12},{12,14},{14,0},{1,3},{3,5},... | collective-permute-start | bytes 393224 | tf_op jit(solution)/shard_map/ppermute | solution.py:335
  22.6 6.2 %collective-permute-start.12 = (f32[64,512]{1,0:T(8,128)S(1)}, f32[64,512]{1,0:T(8,128)S(1)}, u32[]{:S(2)}, u32[]{:S(2)}) collective-permute-start(f32[64,512]{1,0:T(8,128)S(1)} %collective-permute-done.10), channel_id=1, source_target_pairs={{0,14},{2,0},{4,2},{6,4},{8,6},{10,8},{12,10},{14,12},{1,15},{3,1}... | collective-permute-start | bytes 393224 | tf_op jit(solution)/shard_map/ppermute | solution.py:335
  28.7 6.2 %collective-permute-start.14 = (f32[64,512]{1,0:T(8,128)S(1)}, f32[64,512]{1,0:T(8,128)S(1)}, u32[]{:S(2)}, u32[]{:S(2)}) collective-permute-start(f32[64,512]{1,0:T(8,128)S(1)} %collective-permute-done.11), channel_id=1, source_target_pairs={{0,2},{2,4},{4,6},{6,8},{8,10},{10,12},{12,14},{14,0},{1,3},{3,5},... | collective-permute-start | bytes 393224 | tf_op jit(solution)/shard_map/ppermute | solution.py:335
  28.7 6.2 %collective-permute-start.15 = (f32[64,512]{1,0:T(8,128)S(1)}, f32[64,512]{1,0:T(8,128)S(1)}, u32[]{:S(2)}, u32[]{:S(2)}) collective-permute-start(f32[64,512]{1,0:T(8,128)S(1)} %collective-permute-done.12), channel_id=1, source_target_pairs={{0,14},{2,0},{4,2},{6,4},{8,6},{10,8},{12,10},{14,12},{1,15},{3,1}... | collective-permute-start | bytes 393224 | tf_op jit(solution)/shard_map/ppermute | solution.py:335
  34.9 12.8 %collective-permute-start.16 = (f32[32,512]{1,0:T(8,128)S(1)}, f32[32,512]{1,0:T(8,128)S(1)}, u32[]{:S(2)}, u32[]{:S(2)}) collective-permute-start(f32[32,512]{1,0:T(8,128)S(1)} %slice.104), channel_id=1, source_target_pairs={{0,2},{2,4},{4,6},{6,8},{8,10},{10,12},{12,14},{14,0},{1,3},{3,5},... | collective-permute-start | bytes 196616 | tf_op jit(solution)/shard_map/ppermute | solution.py:335
  35.0 12.8 %collective-permute-start.17 = (f32[32,512]{1,0:T(8,128)S(1)}, f32[32,512]{1,0:T(8,128)S(1)}, u32[]{:S(2)}, u32[]{:S(2)}) collective-permute-start(f32[32,512]{1,0:T(8,128)S(1)} %slice.105), channel_id=1, source_target_pairs={{0,14},{2,0},{4,2},{6,4},{8,6},{10,8},{12,10},{14,12},{1,15},{3,1}... | collective-permute-start | bytes 196616 | tf_op jit(solution)/shard_map/ppermute | solution.py:335
  38.3 1.3 copy-start.1
  47.1 20.9 %collective-permute-start = (f32[8,64,512]{2,1,0:T(8,128)}, f32[8,64,512]{2,1,0:T(8,128)}, u32[]{:S(2)}, u32[]{:S(2)}) collective-permute-start(f32[8,64,512]{2,1,0:T(8,128)} %get-tuple-element.18), channel_id=1, source_target_pairs={{0,1},{1,0},{2,3},{3,2},{4,5},{5,4},{6,7},{7,6},{8,9},{9,8},{10,11... | collective-permute-start | bytes 3145736 | tf_op jit(solution)/shard_map/ppermute | solution.py:335
  47.1 4.4 %copy-start.5 = (f32[5,64,512]{2,1,0:T(8,128)}, f32[5,64,512]{2,1,0:T(8,128)S(1)}, u32[]{:S(2)}) copy-start(f32[5,64,512]{2,1,0:T(8,128)S(1)} %bitcast_dynamic-update-slice_fusion.near) | copy-start | bytes 1966084
  47.1 4.3 %collective-permute-start.13 = (f32[5,64,512]{2,1,0:T(8,128)S(1)}, f32[5,64,512]{2,1,0:T(8,128)S(1)}, u32[]{:S(2)}, u32[]{:S(2)}) collective-permute-start(f32[5,64,512]{2,1,0:T(8,128)S(1)} %bitcast_dynamic-update-slice_fusion.near), channel_id=1, source_target_pairs={{0,1},{1,0},{2,3},{3,2},{4,5},{5,4},{6,7},{7,6},{8,9},{9,8},{10,11... | collective-permute-start | bytes 1966088 | tf_op jit(solution)/shard_map/ppermute | solution.py:335
  47.8 3.7 %copy-start.4 = (f32[3,64,512]{2,1,0:T(8,128)}, f32[3,64,512]{2,1,0:T(8,128)S(1)}, u32[]{:S(2)}) copy-start(f32[3,64,512]{2,1,0:T(8,128)S(1)} %pad_maximum_fusion.far) | copy-start | bytes 1179652
  47.8 3.7 %collective-permute-start.18 = (f32[3,64,512]{2,1,0:T(8,128)S(1)}, f32[3,64,512]{2,1,0:T(8,128)S(1)}, u32[]{:S(2)}, u32[]{:S(2)}) collective-permute-start(f32[3,64,512]{2,1,0:T(8,128)S(1)} %pad_maximum_fusion.far), channel_id=1, source_target_pairs={{0,1},{1,0},{2,3},{3,2},{4,5},{5,4},{6,7},{7,6},{8,9},{9,8},{10,11... | collective-permute-start | bytes 1179656 | tf_op jit(solution)/shard_map/ppermute | solution.py:335
  51.5 0.8 copy-start.8
  52.2 0.8 copy-start.7
  60.1 8.0 %copy-start.3 = (f32[8,64,512]{2,1,0:T(8,128)S(1)}, f32[8,64,512]{2,1,0:T(8,128)}, u32[]{:S(2)}) copy-start(f32[8,64,512]{2,1,0:T(8,128)} %get-tuple-element.17) | copy-start | bytes 3145732
  60.1 41.9 %all-to-all-start.1 = ((f32[16,64,512]{2,1,0:T(8,128)}), f32[16,64,512]{2,1,0:T(8,128)S(1)}, u32[]{:S(2)}, u32[]{:S(2)}) async-start(f32[16,64,512]{2,1,0:T(8,128)} %bitcast.66), calls=%async_computation.1 | async-start | bytes 4194304 | tf_op jit(solution)/shard_map/all_to_all | solution.py:382
  69.5 8.4 %collective-permute-start.1 = (f32[32,512]{1,0:T(8,128)S(1)}, f32[32,512]{1,0:T(8,128)S(1)}, u32[]{:S(2)}, u32[]{:S(2)}) collective-permute-start(f32[32,512]{1,0:T(8,128)S(1)} %get-tuple-element.31), channel_id=1, source_target_pairs={{0,2},{2,4},{4,6},{6,8},{8,10},{10,12},{12,14},{14,0},{1,3},{3,5},... | collective-permute-start | bytes 196616 | tf_op jit(solution)/shard_map/ppermute | solution.py:335
  71.7 6.2 %collective-permute-start.5 = (f32[32,512]{1,0:T(8,128)S(1)}, f32[32,512]{1,0:T(8,128)S(1)}, u32[]{:S(2)}, u32[]{:S(2)}) collective-permute-start(f32[32,512]{1,0:T(8,128)S(1)} %get-tuple-element.32), channel_id=1, source_target_pairs={{0,14},{2,0},{4,2},{6,4},{8,6},{10,8},{12,10},{14,12},{1,15},{3,1}... | collective-permute-start | bytes 196616 | tf_op jit(solution)/shard_map/ppermute | solution.py:335
  77.9 6.3 %collective-permute-start.2 = (f32[64,512]{1,0:T(8,128)S(1)}, f32[64,512]{1,0:T(8,128)S(1)}, u32[]{:S(2)}, u32[]{:S(2)}) collective-permute-start(f32[64,512]{1,0:T(8,128)S(1)} %pad_maximum_fusion.1), channel_id=1, source_target_pairs={{0,2},{2,4},{4,6},{6,8},{8,10},{10,12},{12,14},{14,0},{1,3},{3,5},... | collective-permute-start | bytes 393224 | tf_op jit(solution)/shard_map/ppermute | solution.py:335
  78.1 6.3 %collective-permute-start.6 = (f32[64,512]{1,0:T(8,128)S(1)}, f32[64,512]{1,0:T(8,128)S(1)}, u32[]{:S(2)}, u32[]{:S(2)}) collective-permute-start(f32[64,512]{1,0:T(8,128)S(1)} %pad_maximum_fusion.2), channel_id=1, source_target_pairs={{0,14},{2,0},{4,2},{6,4},{8,6},{10,8},{12,10},{14,12},{1,15},{3,1}... | collective-permute-start | bytes 393224 | tf_op jit(solution)/shard_map/ppermute | solution.py:335
  84.3 6.3 %collective-permute-start.3 = (f32[64,512]{1,0:T(8,128)S(1)}, f32[64,512]{1,0:T(8,128)S(1)}, u32[]{:S(2)}, u32[]{:S(2)}) collective-permute-start(f32[64,512]{1,0:T(8,128)S(1)} %fusion.2), channel_id=1, source_target_pairs={{0,2},{2,4},{4,6},{6,8},{8,10},{10,12},{12,14},{14,0},{1,3},{3,5},... | collective-permute-start | bytes 393224 | tf_op jit(solution)/shard_map/ppermute | solution.py:335
  90.6 5.6 %collective-permute-start.7 = (f32[64,512]{1,0:T(8,128)S(1)}, f32[64,512]{1,0:T(8,128)S(1)}, u32[]{:S(2)}, u32[]{:S(2)}) collective-permute-start(f32[64,512]{1,0:T(8,128)S(1)} %get-tuple-element.28), channel_id=1, source_target_pairs={{0,14},{2,0},{4,2},{6,4},{8,6},{10,8},{12,10},{14,12},{1,15},{3,1}... | collective-permute-start | bytes 393224 | tf_op jit(solution)/shard_map/ppermute | solution.py:335
  91.5 6.3 %collective-permute-start.4 = (f32[64,512]{1,0:T(8,128)S(1)}, f32[64,512]{1,0:T(8,128)S(1)}, u32[]{:S(2)}, u32[]{:S(2)}) collective-permute-start(f32[64,512]{1,0:T(8,128)S(1)} %get-tuple-element.27), channel_id=1, source_target_pairs={{0,2},{2,4},{4,6},{6,8},{8,10},{10,12},{12,14},{14,0},{1,3},{3,5},... | collective-permute-start | bytes 393224 | tf_op jit(solution)/shard_map/ppermute | solution.py:335
  96.3 5.0 %collective-permute-start.8 = (f32[64,512]{1,0:T(8,128)S(1)}, f32[64,512]{1,0:T(8,128)S(1)}, u32[]{:S(2)}, u32[]{:S(2)}) collective-permute-start(f32[64,512]{1,0:T(8,128)S(1)} %fusion.1), channel_id=1, source_target_pairs={{0,14},{2,0},{4,2},{6,4},{8,6},{10,8},{12,10},{14,12},{1,15},{3,1}... | collective-permute-start | bytes 393224 | tf_op jit(solution)/shard_map/ppermute | solution.py:335
  102.0 1.3 copy-start
  108.0 3.1 %collective-permute-start.19 = (f32[2304,128]{1,0:T(8,128)}, f32[2304,128]{1,0:T(8,128)S(1)}, u32[]{:S(2)}, u32[]{:S(2)}) collective-permute-start(f32[2304,128]{1,0:T(8,128)} %get-tuple-element.20), channel_id=1, source_target_pairs={{0,1},{1,0},{2,3},{3,2},{4,5},{5,4},{6,7},{7,6},{8,9},{9,8},{10,11... | collective-permute-start | bytes 3538952 | tf_op jit(solution)/shard_map/ppermute | solution.py:335
  181.5 13.1 %copy-start.2 = (f32[16,144,128]{2,1,0:T(8,128)}, f32[16,144,128]{2,1,0:T(8,128)S(1)}, u32[]{:S(2)}) copy-start(f32[16,144,128]{2,1,0:T(8,128)S(1)} %all_to_all.27) | copy-start | bytes 3538948
  181.5 24.7 %collective-permute-start.20 = (f32[2304,128]{1,0:T(8,128)S(1)}, f32[2304,128]{1,0:T(8,128)S(1)}, u32[]{:S(2)}, u32[]{:S(2)}) collective-permute-start(f32[2304,128]{1,0:T(8,128)S(1)} %bitcast.68), channel_id=1, source_target_pairs={{0,1},{1,0},{2,3},{3,2},{4,5},{5,4},{6,7},{7,6},{8,9},{9,8},{10,11... | collective-permute-start | bytes 3538952 | tf_op jit(solution)/shard_map/ppermute | solution.py:335
  206.2 1.0 copy-start.6

commit v2 on v1

--- a/solution.py
+++ b/solution.py
@@ -36,7 +36,7 @@
     )
 
 
-def call(kernel, outs, flops, grid=None, in_specs=None, out_specs=None, scratch=()):
+def call(kernel, outs, flops, grid=None, in_specs=None, out_specs=None, scratch=(), limit=None):
     specs = {} if grid is None else {"grid": grid}
     return pl.pallas_call(
         kernel,
@@ -44,6 +44,7 @@
         in_specs=in_specs,
         out_specs=out_specs,
         scratch_shapes=scratch,
+        compiler_params=pltpu.CompilerParams(vmem_limit_bytes=limit),
         cost_estimate=pl.CostEstimate(flops=flops, bytes_accessed=8 * 2**20, transcendentals=0),
         **specs,
     )
@@ -51,6 +52,14 @@
 
 def array(*shape):
     return jax.ShapeDtypeStruct(shape, F32)
+
+
+def near_core(*values):
+    return tuple(pltpu.with_memory_space_constraint(v, pltpu.VMEM) for v in values)
+
+
+def far_core(*values):
+    return tuple(pltpu.with_memory_space_constraint(v, pltpu.HBM) for v in values)
 
 
 def matmul(left_side, right_side, dims=NN):
@@ -104,7 +113,7 @@
     return call(
         invert_kernel, array(*factor_diag.shape), 10**10,
         in_specs=[VMEM], out_specs=VMEM, scratch=[blocks, blocks],
-    )(factor_diag)
+    )(*far_core(factor_diag))
 
 
 def constants_kernel(factor, mid, adjoint, adjoint_mid, inverses, solved, second, first):
@@ -118,24 +127,25 @@
     return call(
         constants_kernel, (square, square, square), 5 * 10**9,
         in_specs=[VMEM] * 5, out_specs=(VMEM,) * 3,
-    )(factor_diag, factor_mid, adjoint_diag, adjoint_mid, inverses)
+    )(*far_core(factor_diag, factor_mid, adjoint_diag, adjoint_mid, inverses))
 
 
 def turn_kernel(block, high, low):
     high[...], low[...] = split(block[...].T)
 
 
-def turn(flipped):
+def turn(flipped, part):
     count, depth = flipped.shape
-    step = min(256, depth)
-    out = jax.ShapeDtypeStruct((depth, count), BF16)
+    step = min(256, depth // 2)
+    steps = depth // 2 // step
+    out = jax.ShapeDtypeStruct((depth // 2, count), BF16)
     tall = pl.BlockSpec((step, count), lambda i: (i, 0))
     return call(
         turn_kernel, (out, out), 10**9,
-        grid=(depth // step,),
-        in_specs=[pl.BlockSpec((count, step), lambda i: (0, i))],
+        grid=(steps,),
+        in_specs=[pl.BlockSpec((count, step), lambda i: (0, part * steps + i))],
         out_specs=(tall, tall),
-    )(flipped)
+    )(*far_core(flipped))
 
 
 def first_image_kernel(offsets, place, block, near, near_other, far, far_other, out, high, low):
@@ -160,52 +170,40 @@
     count, depth = flipped.shape
     size = near.shape[2]
     step = min(512, count)
-    whole = lambda v: pl.BlockSpec(v.shape, lambda i: (0, 0, 0), pipeline_mode=pl.Buffered(1))
-    gathered = (near, near_other, far, far_other)
-    return call(
-        functools.partial(first_image_kernel, offsets), array(count, size), 3 * 10**9,
+    gathered = near_core(near, near_other, far, far_other)
+    return call(
+        functools.partial(first_image_kernel, offsets), array(count, size), 3 * 10**9, limit=32 * 2**20,
         grid=(count // step,),
-        in_specs=[SMEM, pl.BlockSpec((step, depth), lambda i: (i, 0))] + [whole(v) for v in gathered],
+        in_specs=[SMEM, pl.BlockSpec((step, depth), lambda i: (i, 0))] + [VMEM] * 4,
         out_specs=pl.BlockSpec((step, size), lambda i: (i, 0)),
         scratch=[pltpu.VMEM((depth, size), BF16)] * 2,
-    )(place, flipped, *gathered)
-
-
-def second_image_kernel(place, high, low, columns, keep, give, right_high, right_low):
+    )(place, *far_core(flipped), *gathered)
+
+
+def second_image_kernel(place, *refs):
+    turned, (columns, keep, give) = refs[:-3], refs[-3:]
     chip, core = place[0], place[1]
     rows = keep.shape[1]
-
-    @pl.when(pl.program_id(0) == 0)
-    def _():
-        right_high[...], right_low[...] = split(columns[...])
-
-    value = pair_product((high[...], low[...]), (right_high[...], right_low[...]))
-    chips = value.shape[0] // (2 * rows)
-    for n in range(chips):
-        slot = lax.rem(pl.program_id(0) * chips + n - chip + SIZES["z"], SIZES["z"])
-        even = value[2 * n * rows : (2 * n + 1) * rows, :]
-        odd = value[(2 * n + 1) * rows : (2 * n + 2) * rows, :]
-        keep[slot] = jnp.where(core == 0, even, odd)
-        give[slot] = jnp.where(core == 0, odd, even)
-
-
-def second_image(place, high, low, columns):
-    depth, count = high.shape
-    size = columns.shape[1]
-    step = min(512, depth)
-    tall = pl.BlockSpec((step, count), lambda i: (i, 0))
-    rows = depth // (2 * SIZES["z"])
-    out = array(SIZES["z"], rows, size)
-    spec = pl.BlockSpec(out.shape, lambda i: (0, 0, 0))
-    return call(
-        second_image_kernel, (out, out), 3 * 10**9,
-        grid=(depth // step,),
-        in_specs=[
-            SMEM, tall, tall, pl.BlockSpec((count, size), lambda i: (0, 0), pipeline_mode=pl.Buffered(1)),
-        ],
-        out_specs=(spec, spec),
-        scratch=[pltpu.VMEM((count, size), BF16)] * 2,
-    )(place, high, low, columns)
+    right = split(columns[...])
+    for part in range(len(turned) // 2):
+        value = pair_product((turned[2 * part][...], turned[2 * part + 1][...]), right)
+        chips = value.shape[0] // (2 * rows)
+        for n in range(chips):
+            slot = lax.rem(part * chips + n - chip + SIZES["z"], SIZES["z"])
+            even = value[2 * n * rows : (2 * n + 1) * rows, :]
+            odd = value[(2 * n + 1) * rows : (2 * n + 2) * rows, :]
+            keep[slot] = jnp.where(core == 0, even, odd)
+            give[slot] = jnp.where(core == 0, odd, even)
+
+
+def second_image(place, turned, columns):
+    depth, size = 2 * turned[0].shape[0], columns.shape[1]
+    out = array(SIZES["z"], depth // (2 * SIZES["z"]), size)
+    return call(
+        second_image_kernel, (out, out), 3 * 10**9, limit=32 * 2**20,
+        in_specs=[SMEM] + [VMEM] * (len(turned) + 1),
+        out_specs=(VMEM, VMEM),
+    )(place, *far_core(*turned), *near_core(columns))
 
 
 def terms_kernel(place, second_sum, pieces, adjoint, factor, keep, give, rows, second_second, second_first, first_first):
@@ -259,11 +257,11 @@
     per = size // TILE
     half = per * (2 * per + 1) // 2 * TILE
     return call(
-        terms_kernel, (array(half, TILE), array(half, TILE), array(*adjoint_low.shape)), 10**9,
+        terms_kernel, (array(half, TILE), array(half, TILE), array(*adjoint_low.shape)), 10**9, limit=32 * 2**20,
         in_specs=[SMEM] + [VMEM] * 4,
         out_specs=(VMEM,) * 3,
         scratch=[pltpu.VMEM((size, size), F32)] * 3,
-    )(place, second_sum, pieces, adjoint_low, factor_low)
+    )(place, *near_core(second_sum, pieces), *far_core(adjoint_low, factor_low))
 
 
 def rows_kernel(rows, inverses, solved, out):
@@ -306,28 +304,67 @@
     for i in range(per):
         for j in range(per):
             cross[at(i, j)] = tile(low + i * per + j)
-    known = solved[...]
-    image = matmul(second[...], known)
-    outer = matmul(known, 0.5 * image + cross[...], TN)
+    middle = size // 2
+    whole, top_half, low_half = slice(0, size), slice(0, middle), slice(middle, size)
+
+    def part(pair, rows, cols):
+        return tuple(v[rows, cols] for v in pair)
+
+    def times_lower(left, lower):
+        return jnp.concatenate(
+            [
+                pair_product(left, part(lower, whole, top_half)),
+                pair_product(part(left, whole, low_half), part(lower, low_half, low_half)),
+            ],
+            axis=1,
+        )
+
+    def upper_times(upper, right):
+        return jnp.concatenate(
+            [
+                pair_product(part(upper, top_half, whole), right),
+                pair_product(part(upper, low_half, low_half), part(right, low_half, whole)),
+            ]
+        )
+
+    def between(upper, symmetric, lower, out):
+        half_way = split(times_lower(symmetric, lower))
+        out[top_half, top_half] = 0.5 * pair_product(
+            part(upper, top_half, whole), part(half_way, whole, top_half)
+        )
+        bottom = 0.5 * pair_product(
+            part(upper, low_half, low_half), part(half_way, low_half, whole)
+        )
+        out[low_half, whole] = bottom
+        out[top_half, low_half] = bottom[:, top_half].T
+
+    first_lower, second_lower = split(inverses[0]), split(inverses[1])
+    first_upper, second_upper = split(inverses[0].T), split(inverses[1].T)
+    second_symmetric = split(second[...])
+    image = pair_product(second_symmetric, split(solved[...]))
+    outer = pair_product(split(solved[...].T), split(0.5 * image + cross[...]))
     outer = outer + outer.T
 
     def first_value(i, j):
         return first_const[at(i, j)] - tile(low + per * per + number(i, j)) + outer[at(i, j)]
 
     mirror(first_value, first)
-    diag[0] = 0.5 * matmul(matmul(inverses[0], first[...], TN), inverses[0])
-    diag[1] = 0.5 * matmul(matmul(inverses[1], second[...], TN), inverses[1])
-    rest = adjoint_mid[...] - matmul(inverses[1], image + cross[...], TN)
-    top[...] = 0.5 * matmul(rest, inverses[0])
+    between(first_upper, split(first[...]), first_lower, diag.at[0])
+    between(second_upper, second_symmetric, second_lower, diag.at[1])
+    rest = adjoint_mid[...] - upper_times(second_upper, split(image + cross[...]))
+    top[...] = 0.5 * times_lower(split(rest), first_lower)
 
 
 def finish(place, tiles, other, inverses, mid_solved, second_const, first_const, adjoint_mid):
     size = mid_solved.shape[0]
     return call(
-        finish_kernel, (array(2, size, size), array(size, size)), 10**10,
+        finish_kernel, (array(2, size, size), array(size, size)), 10**10, limit=32 * 2**20,
         in_specs=[SMEM] + [VMEM] * 7, out_specs=(VMEM, VMEM),
         scratch=[pltpu.VMEM((size, size), F32)] * 3,
-    )(place, tiles, other, inverses, mid_solved, second_const, first_const, adjoint_mid)
+    )(
+        place, *near_core(tiles, other),
+        *far_core(inverses, mid_solved, second_const, first_const, adjoint_mid),
+    )
 
 
 def shift(value, axis, step):
@@ -339,7 +376,8 @@
     size = SIZES[axis]
     far = blocks[size // 2]
     half = far.shape[0] // 2
-    ahead, behind = shift(far[:half], axis, 1), shift(far[half:], axis, -1)
+    ahead = shift(far[:half], axis, 1)
+    behind = shift(far[half:], axis, -1)
     for step in range(size // 2 - 1, 0, -1):
         up, down = blocks[step], blocks[size - step]
         if step == size // 2 - 1:
@@ -375,13 +413,16 @@
     across = jnp.concatenate([shift(ahead[3][:half], "z", 1), shift(behind[3][half:], "z", -1)])
     near = jnp.stack([own, ahead[1], behind[1], ahead[2], behind[2]])
     far = jnp.stack([ahead[3], behind[3], across])
-    high, low = turn(flipped)
+    near_other, far_other = shift(near, "c", 1), shift(far, "c", 1)
+    turned = turn(flipped, 0)
+    turned += turn(flipped, 1)
     images = first_image(
-        (0, -1, 1, -2, 2, -3, 3, 4), place, flipped, near, shift(near, "c", 1), far, shift(far, "c", 1)
+        (0, -1, 1, -2, 2, -3, 3, 4), place, flipped, near, near_other, far, far_other
     )
     pieces = lax.all_to_all(images.reshape(parts, rows, size), ("y", "x"), 0, 0)
-    keep, give = second_image(place, high, low, columns)
-    second_sum = ring_sum(keep + shift(give, "c", 1), "z")
+    keep, give = second_image(place, turned, columns)
+    give = shift(give, "c", 1)
+    second_sum = ring_sum(keep + give, "z")
 
     keep, give, sides = terms(place, second_sum, pieces, adjoint_low, factor_low)
     keep = keep + shift(give, "c", 1)
@@ -395,7 +436,7 @@
     )
     low = call(
         rows_kernel, array(2, rows, size), 10**9, in_specs=[VMEM] * 3, out_specs=VMEM
-    )(sides, inverses, mid_solved)
+    )(*far_core(sides, inverses, mid_solved))
     diag, top = finish(place, tiles, other, inverses, mid_solved, second_const, first_const, adjoint_mid)
     return diag, top, low
 

time: 222 us -> 209 us (0.941)
  Pallas kernels: 61 us -> 55.3 us
  local copies, waits for them, and re-layouts: 8.07 us -> 5.36 us
    unnamed x21 -> x11, local copies, waits for them, and re-layouts: 5.31 us -> 1.36 us
    pallas_call x2 -> x3, Pallas kernels: 12.8 us -> 12.6 us  [the longest x1 6.63 us: second_image(): call(second_image_kernel, (out, out), 3 * 10 ** 9, limit=32 * 2 ** 20, in...]
  transfers between devices with their start and end apart: 23 -> 23, of which waited for: 9 -> 9; matrix products, arithmetic and copies ran while one was open for 1% -> 2% of each run, Pallas kernels for 20% -> 20%
where the time goes in v2:
time: 209 us; the launch traced here: 206 us
  blocking collectives  68.8 us (33%)
  Pallas kernels  55.3 us (26%)
  starting transfers between devices  43.8 us (21%)
  waiting for transfers between devices  29.4 us (14%)
  local copies, waits for them, and re-layouts  5.36 us (3%)
  other arithmetic  2.78 us (1%)
    all_to_all x2, blocking collectives, spread(): lax.all_to_all(jnp.broadcast_to(value[None], (parts,) + value.shape), axe...  44.1 us
    ppermute x21, waiting for transfers between devices, shift(): lax.ppermute(value, axis, [(i, (i + step) % size) for i in range(size)])  29.4 us
    ppermute x21, starting transfers between devices, shift(): lax.ppermute(value, axis, [(i, (i + step) % size) for i in range(size)])  29.1 us
    all_to_all x1, blocking collectives, shards(): tiles = lax.all_to_all(keep.reshape(parts, -1, TILE), ('y', 'x'), 0, 0)  24.7 us
    pallas_call x1, Pallas kernels, invert(): call(invert_kernel, array(*factor_diag.shape), 10 ** 10, in_specs=[VMEM],...  12.5 us
    pallas_call x1, Pallas kernels, finish(): call(finish_kernel, (array(2, size, size), array(size, size)), 10 ** 10,...  10.6 us
    pallas_call x1, Pallas kernels, constants(): call(constants_kernel, (square, square, square), 5 * 10 ** 9, in_specs=[V...  7.93 us
    all_to_all x1, starting transfers between devices, spread(): lax.all_to_all(jnp.broadcast_to(value[None], (parts,) + value.shape), axe...  7.48 us
  transfers between devices with their start and end apart: 23, of which 9 were waited for; matrix products, arithmetic and copies ran while one was open for 2% of the time, Pallas kernels for 20%

profile of v2, /device:TPU:2, one launch (start us, length us, event | category | flops | bytes accessed | tf_op | source)
XLA Modules:
  0.0 206.4 jit_solution(13499706178740805660)
XLA Ops:
  1.6 1.6 broadcast_in_dim.9
  3.2 7.5 %all-to-all-start = ((f32[16,64,512]{2,1,0:T(8,128)}), f32[16,64,512]{2,1,0:T(8,128)S(1)}, u32[]{:S(2)}, u32[]{:S(2)}) async-start(f32[16,64,512]{2,1,0:T(8,128)} %broadcast_in_dim.9), calls=%async_computation | async-start | bytes 4194304 | tf_op jit(solution)/shard_map/all_to_all | solution.py:393
  10.7 1.9 collective-permute-start.9
  12.6 4.0 %collective-permute-start.10 = (f32[64,512]{1,0:T(8,128)S(1)}, f32[64,512]{1,0:T(8,128)S(1)}, u32[]{:S(2)}, u32[]{:S(2)}) collective-permute-start(f32[64,512]{1,0:T(8,128)S(1)} %get-tuple-element.39), channel_id=1, source_target_pairs={{0,14},{2,0},{4,2},{6,4},{8,6},{10,8},{12,10},{14,12},{1,15},{3,1}... | collective-permute-start | bytes 393224 | tf_op jit(solution)/shard_map/ppermute | solution.py:372
  16.6 3.0 %shard_map.94 = (bf16[512,1024]{1,0:T(8,128)(2,1)}, bf16[512,1024]{1,0:T(8,128)(2,1)}) custom-call(f32[1024,1024]{1,0:T(8,128)} %bitcast.67), custom_call_target="tpu_custom_call" | custom-call | flops 1000000000 | bytes 8388608 | tf_op jit(solution)/shard_map/pallas_call | solution.py:143
  19.6 3.0 %shard_map.95 = (bf16[512,1024]{1,0:T(8,128)(2,1)}, bf16[512,1024]{1,0:T(8,128)(2,1)}) custom-call(f32[1024,1024]{1,0:T(8,128)} %bitcast.68), custom_call_target="tpu_custom_call" | custom-call | flops 1000000000 | bytes 8388608 | tf_op jit(solution)/shard_map/pallas_call | solution.py:143
  22.7 3.2 %collective-permute-start.12 = (f32[64,512]{1,0:T(8,128)S(1)}, f32[64,512]{1,0:T(8,128)S(1)}, u32[]{:S(2)}, u32[]{:S(2)}) collective-permute-start(f32[64,512]{1,0:T(8,128)S(1)} %collective-permute-done.10), channel_id=1, source_target_pairs={{0,14},{2,0},{4,2},{6,4},{8,6},{10,8},{12,10},{14,12},{1,15},{3,1}... | collective-permute-start | bytes 393224 | tf_op jit(solution)/shard_map/ppermute | solution.py:372
  26.0 2.9 %collective-permute-done.11 = f32[64,512]{1,0:T(8,128)S(1)} collective-permute-done((f32[64,512]{1,0:T(8,128)S(1)}, f32[64,512]{1,0:T(8,128)S(1)}, u32[]{:S(2)}, u32[]{:S(2)}) %collective-permute-start.11) | collective-permute-done | bytes 131104 | tf_op jit(solution)/shard_map/ppermute | solution.py:372
  28.9 3.2 %collective-permute-start.15 = (f32[64,512]{1,0:T(8,128)S(1)}, f32[64,512]{1,0:T(8,128)S(1)}, u32[]{:S(2)}, u32[]{:S(2)}) collective-permute-start(f32[64,512]{1,0:T(8,128)S(1)} %collective-permute-done.12), channel_id=1, source_target_pairs={{0,14},{2,0},{4,2},{6,4},{8,6},{10,8},{12,10},{14,12},{1,15},{3,1}... | collective-permute-start | bytes 393224 | tf_op jit(solution)/shard_map/ppermute | solution.py:372
  32.1 2.9 %collective-permute-done.14 = f32[64,512]{1,0:T(8,128)S(1)} collective-permute-done((f32[64,512]{1,0:T(8,128)S(1)}, f32[64,512]{1,0:T(8,128)S(1)}, u32[]{:S(2)}, u32[]{:S(2)}) %collective-permute-start.14) | collective-permute-done | bytes 131104 | tf_op jit(solution)/shard_map/ppermute | solution.py:372
  36.3 3.2 %collective-permute-start.17 = (f32[32,512]{1,0:T(8,128)}, f32[32,512]{1,0:T(8,128)}, u32[]{:S(2)}, u32[]{:S(2)}) collective-permute-start(f32[32,512]{1,0:T(8,128)} %slice.105), channel_id=1, source_target_pairs={{0,14},{2,0},{4,2},{6,4},{8,6},{10,8},{12,10},{14,12},{1,15},{3,1}... | collective-permute-start | bytes 196616 | tf_op jit(solution)/shard_map/ppermute | solution.py:372
  39.6 6.6 %shard_map.96 = (f32[8,64,512]{2,1,0:T(8,128)S(1)}, f32[8,64,512]{2,1,0:T(8,128)}) custom-call(s32[2]{0:T(128)S(1)} %pad_add_fusion.place, bf16[512,1024]{1,0:T(8,128)(2,1)} %get-tuple-element.17.refs_0_, bf16[512,1024]{1,0:T(8,128)(2,1)} %get-tuple-element.18.refs_1_, bf16[512,1024]{1,0:T(8,128)(2,1)} %get-tuple-element.19.refs_2_, ...), custom_call_target="tpu_custom_call" | custom-call | flops 3000000000 | bytes 8388608 | tf_op jit(solution)/shard_map/pallas_call | solution.py:202
  48.0 2.5 %collective-permute-done.18.far_other = f32[3,64,512]{2,1,0:T(8,128)S(1)} collective-permute-done((f32[3,64,512]{2,1,0:T(8,128)S(1)}, f32[3,64,512]{2,1,0:T(8,128)S(1)}, u32[]{:S(2)}, u32[]{:S(2)}) %collective-permute-start.18) | collective-permute-done | bytes 393248 | tf_op jit(solution)/shard_map/ppermute | solution.py:372
  50.6 5.5 %shard_map.97 = f32[1024,512]{1,0:T(8,128)S(1)} custom-call(s32[2]{0:T(128)S(1)} %pad_add_fusion.place, f32[1024,1024]{1,0:T(8,128)} %bitcast.69, f32[5,64,512]{2,1,0:T(8,128)S(1)} %bitcast_dynamic-update-slice_fusion.near, f32[5,64,512]{2,1,0:T(8,128)S(1)} %collective-permute-done.13.near_other, f32[3,64,512]{2,1,0:T(8,128)S(1)} %pad_maximum_fusion.far, ...), custom_call_target="tpu_custom_call" | custom-call | flops 3000000000 | bytes 8388608 | tf_op jit(solution)/shard_map/pallas_call | solution.py:174
  57.4 7.2 %all-to-all-start.1 = ((f32[16,64,512]{2,1,0:T(8,128)}), f32[16,64,512]{2,1,0:T(8,128)S(1)}, u32[]{:S(2)}, u32[]{:S(2)}) async-start(f32[16,64,512]{2,1,0:T(8,128)} %bitcast.63), calls=%async_computation.1 | async-start | bytes 4194304 | tf_op jit(solution)/shard_map/all_to_all | solution.py:422
  67.4 4.0 %collective-permute-start.5 = (f32[32,512]{1,0:T(8,128)S(1)}, f32[32,512]{1,0:T(8,128)S(1)}, u32[]{:S(2)}, u32[]{:S(2)}) collective-permute-start(f32[32,512]{1,0:T(8,128)S(1)} %get-tuple-element.36), channel_id=1, source_target_pairs={{0,14},{2,0},{4,2},{6,4},{8,6},{10,8},{12,10},{14,12},{1,15},{3,1}... | collective-permute-start | bytes 196616 | tf_op jit(solution)/shard_map/ppermute | solution.py:372
  71.4 2.2 %collective-permute-done.1 = f32[32,512]{1,0:T(8,128)S(1)} collective-permute-done((f32[32,512]{1,0:T(8,128)S(1)}, f32[32,512]{1,0:T(8,128)S(1)}, u32[]{:S(2)}, u32[]{:S(2)}) %collective-permute-start.1) | collective-permute-done | bytes 65568 | tf_op jit(solution)/shard_map/ppermute | solution.py:372
  73.7 3.4 %collective-permute-start.6 = (f32[64,512]{1,0:T(8,128)S(1)}, f32[64,512]{1,0:T(8,128)S(1)}, u32[]{:S(2)}, u32[]{:S(2)}) collective-permute-start(f32[64,512]{1,0:T(8,128)S(1)} %pad_maximum_fusion.2), channel_id=1, source_target_pairs={{0,14},{2,0},{4,2},{6,4},{8,6},{10,8},{12,10},{14,12},{1,15},{3,1}... | collective-permute-start | bytes 393224 | tf_op jit(solution)/shard_map/ppermute | solution.py:372
  77.1 2.8 %collective-permute-done.2 = f32[64,512]{1,0:T(8,128)S(1)} collective-permute-done((f32[64,512]{1,0:T(8,128)S(1)}, f32[64,512]{1,0:T(8,128)S(1)}, u32[]{:S(2)}, u32[]{:S(2)}) %collective-permute-start.2) | collective-permute-done | bytes 131104 | tf_op jit(solution)/shard_map/ppermute | solution.py:372
  80.1 6.2 %collective-permute-done.3 = f32[64,512]{1,0:T(8,128)S(1)} collective-permute-done((f32[64,512]{1,0:T(8,128)S(1)}, f32[64,512]{1,0:T(8,128)S(1)}, u32[]{:S(2)}, u32[]{:S(2)}) %collective-permute-start.3) | collective-permute-done | bytes 131104 | tf_op jit(solution)/shard_map/ppermute | solution.py:372
  88.4 3.5 %collective-permute-done.7 = f32[64,512]{1,0:T(8,128)S(1)} collective-permute-done((f32[64,512]{1,0:T(8,128)S(1)}, f32[64,512]{1,0:T(8,128)S(1)}, u32[]{:S(2)}, u32[]{:S(2)}) %collective-permute-start.7) | collective-permute-done | bytes 131104 | tf_op jit(solution)/shard_map/ppermute | solution.py:372
  91.9 1.5 collective-permute-start.8
  93.4 3.5 %collective-permute-done.8 = f32[64,512]{1,0:T(8,128)S(1)} collective-permute-done((f32[64,512]{1,0:T(8,128)S(1)}, f32[64,512]{1,0:T(8,128)S(1)}, u32[]{:S(2)}, u32[]{:S(2)}) %collective-permute-start.8) | collective-permute-done | bytes 131104 | tf_op jit(solution)/shard_map/ppermute | solution.py:372
  97.0 2.5 %shard_map.98 = (f32[2304,128]{1,0:T(8,128)S(1)}, f32[2304,128]{1,0:T(8,128)S(1)}, f32[2,64,512]{2,1,0:T(8,128)S(1)}) custom-call(s32[2]{0:T(128)S(1)} %pad_add_fusion.place, f32[64,512]{1,0:T(8,128)S(1)} %fusion.5.second_sum, f32[16,64,512]{2,1,0:T(8,128)S(1)} %all-to-all-done.1.pieces, f32[2,64,512]{2,1,0:T(8,128)} %adjoint.2, f32[2,64,512]{2,1,0:T(8,128)} %factor.3), custom_call_target="tpu_custom_call" | custom-call | flops 1000000000 | bytes 8388608 | tf_op jit(solution)/shard_map/pallas_call | solution.py:259
  99.6 2.8 %collective-permute-done.19 = f32[2304,128]{1,0:T(8,128)S(1)} collective-permute-done((f32[2304,128]{1,0:T(8,128)S(1)}, f32[2304,128]{1,0:T(8,128)S(1)}, u32[]{:S(2)}, u32[]{:S(2)}) %collective-permute-start.19) | collective-permute-done | bytes 1179680 | tf_op jit(solution)/shard_map/ppermute | solution.py:372
  102.6 24.7 %all_to_all.25 = f32[16,144,128]{2,1,0:T(8,128)S(1)} all-to-all(f32[16,144,128]{2,1,0:T(8,128)S(1)} %bitcast.70), channel_id=1, replica_groups=mesh['y'=4,'x'=4,'z'=8,'c'=2] {'y','x'}, dimensions={0} | all-to-all | bytes 2359296 | tf_op jit(solution)/shard_map/all_to_all | solution.py:429
  127.4 23.7 %all_to_all.26 = f32[8,144,128]{2,1,0:T(8,128)S(1)} all-to-all(f32[8,144,128]{2,1,0:T(8,128)S(1)} %broadcast_in_dim.10), channel_id=1, replica_groups=mesh['y'=4,'x'=4,'z'=8,'c'=2] {'z'}, dimensions={0} | all-to-all | bytes 1179648 | tf_op jit(solution)/shard_map/all_to_all | solution.py:393
  151.3 20.4 %all_to_all.27 = f32[16,144,128]{2,1,0:T(8,128)S(1)} all-to-all(f32[16,144,128]{2,1,0:T(8,128)S(1)} %broadcast_in_dim.22), channel_id=1, replica_groups=mesh['y'=4,'x'=4,'z'=8,'c'=2] {'y','x'}, dimensions={0} | all-to-all | bytes 2359296 | tf_op jit(solution)/shard_map/all_to_all | solution.py:393
  171.6 12.5 %shard_map.99.inverses = f32[2,512,512]{2,1,0:T(8,128)} custom-call(f32[2,512,512]{2,1,0:T(8,128)} %factor.5), custom_call_target="tpu_custom_call" | custom-call | flops 10000000000 | bytes 8388608 | tf_op jit(solution)/shard_map/pallas_call | solution.py:113
  184.1 7.9 %shard_map.100 = (f32[512,512]{1,0:T(8,128)}, f32[512,512]{1,0:T(8,128)}, f32[512,512]{1,0:T(8,128)}) custom-call(f32[2,512,512]{2,1,0:T(8,128)} %factor.5, f32[512,512]{1,0:T(8,128)} %mid.1, f32[2,512,512]{2,1,0:T(8,128)} %adjoint.3, f32[512,512]{1,0:T(8,128)} %adjoint_mid.3, f32[2,512,512]{2,1,0:T(8,128)} %shard_map.99.inverses), custom_call_target="tpu_custom_call" | custom-call | flops 5000000000 | bytes 8388608 | tf_op jit(solution)/shard_map/pallas_call | solution.py:127
  192.1 3.7 %shard_map.102 = f32[2,64,512]{2,1,0:T(8,128)} custom-call(f32[2,64,512]{2,1,0:T(8,128)} %copy-done.3, f32[2,512,512]{2,1,0:T(8,128)} %shard_map.99.inverses, f32[512,512]{1,0:T(8,128)} %get-tuple-element.25.solved), custom_call_target="tpu_custom_call" | custom-call | flops 1000000000 | bytes 8388608 | tf_op jit(solution)/shard_map/pallas_call | solution.py:437
  195.8 10.6 %shard_map.101 = (f32[2,512,512]{2,1,0:T(8,128)}, f32[512,512]{1,0:T(8,128)}) custom-call(s32[2]{0:T(128)S(1)} %pad_add_fusion.place, f32[2304,128]{1,0:T(8,128)S(1)} %bitcast.66, f32[2304,128]{1,0:T(8,128)S(1)} %collective-permute-done.20.other, f32[2,512,512]{2,1,0:T(8,128)} %shard_map.99.inverses, f32[512,512]{1,0:T(8,128)} %get-tuple-element.25.solved, ...), custom_call_target="tpu_custom_call" | custom-call | flops 10000000000 | bytes 8388608 | tf_op jit(solution)/shard_map/pallas_call | solution.py:360
  (59 shorter events, 11.2 us)
Async XLA Ops:
  3.2 36.3 %all-to-all-start = ((f32[16,64,512]{2,1,0:T(8,128)}), f32[16,64,512]{2,1,0:T(8,128)S(1)}, u32[]{:S(2)}, u32[]{:S(2)}) async-start(f32[16,64,512]{2,1,0:T(8,128)} %broadcast_in_dim.9), calls=%async_computation | async-start | bytes 4194304 | tf_op jit(solution)/shard_map/all_to_all | solution.py:393
  10.7 12.0 %collective-permute-start.9 = (f32[64,512]{1,0:T(8,128)S(1)}, f32[64,512]{1,0:T(8,128)S(1)}, u32[]{:S(2)}, u32[]{:S(2)}) collective-permute-start(f32[64,512]{1,0:T(8,128)S(1)} %get-tuple-element.39), channel_id=1, source_target_pairs={{0,2},{2,4},{4,6},{6,8},{8,10},{10,12},{12,14},{14,0},{1,3},{3,5},... | collective-permute-start | bytes 393224 | tf_op jit(solution)/shard_map/ppermute | solution.py:372
  12.6 10.1 %collective-permute-start.10 = (f32[64,512]{1,0:T(8,128)S(1)}, f32[64,512]{1,0:T(8,128)S(1)}, u32[]{:S(2)}, u32[]{:S(2)}) collective-permute-start(f32[64,512]{1,0:T(8,128)S(1)} %get-tuple-element.39), channel_id=1, source_target_pairs={{0,14},{2,0},{4,2},{6,4},{8,6},{10,8},{12,10},{14,12},{1,15},{3,1}... | collective-permute-start | bytes 393224 | tf_op jit(solution)/shard_map/ppermute | solution.py:372
  22.7 6.2 %collective-permute-start.11 = (f32[64,512]{1,0:T(8,128)S(1)}, f32[64,512]{1,0:T(8,128)S(1)}, u32[]{:S(2)}, u32[]{:S(2)}) collective-permute-start(f32[64,512]{1,0:T(8,128)S(1)} %collective-permute-done.9), channel_id=1, source_target_pairs={{0,2},{2,4},{4,6},{6,8},{8,10},{10,12},{12,14},{14,0},{1,3},{3,5},... | collective-permute-start | bytes 393224 | tf_op jit(solution)/shard_map/ppermute | solution.py:372
  22.7 6.2 %collective-permute-start.12 = (f32[64,512]{1,0:T(8,128)S(1)}, f32[64,512]{1,0:T(8,128)S(1)}, u32[]{:S(2)}, u32[]{:S(2)}) collective-permute-start(f32[64,512]{1,0:T(8,128)S(1)} %collective-permute-done.10), channel_id=1, source_target_pairs={{0,14},{2,0},{4,2},{6,4},{8,6},{10,8},{12,10},{14,12},{1,15},{3,1}... | collective-permute-start | bytes 393224 | tf_op jit(solution)/shard_map/ppermute | solution.py:372
  28.9 6.2 %collective-permute-start.14 = (f32[64,512]{1,0:T(8,128)S(1)}, f32[64,512]{1,0:T(8,128)S(1)}, u32[]{:S(2)}, u32[]{:S(2)}) collective-permute-start(f32[64,512]{1,0:T(8,128)S(1)} %collective-permute-done.11), channel_id=1, source_target_pairs={{0,2},{2,4},{4,6},{6,8},{8,10},{10,12},{12,14},{14,0},{1,3},{3,5},... | collective-permute-start | bytes 393224 | tf_op jit(solution)/shard_map/ppermute | solution.py:372
  28.9 6.8 %collective-permute-start.15 = (f32[64,512]{1,0:T(8,128)S(1)}, f32[64,512]{1,0:T(8,128)S(1)}, u32[]{:S(2)}, u32[]{:S(2)}) collective-permute-start(f32[64,512]{1,0:T(8,128)S(1)} %collective-permute-done.12), channel_id=1, source_target_pairs={{0,14},{2,0},{4,2},{6,4},{8,6},{10,8},{12,10},{14,12},{1,15},{3,1}... | collective-permute-start | bytes 393224 | tf_op jit(solution)/shard_map/ppermute | solution.py:372
  32.1 7.4 %copy-start.1 = (f32[5,64,512]{2,1,0:T(8,128)}, f32[5,64,512]{2,1,0:T(8,128)S(1)}, u32[]{:S(2)}) copy-start(f32[5,64,512]{2,1,0:T(8,128)S(1)} %bitcast_dynamic-update-slice_fusion.1) | copy-start | bytes 1966084
  35.7 11.1 %collective-permute-start.16 = (f32[32,512]{1,0:T(8,128)}, f32[32,512]{1,0:T(8,128)}, u32[]{:S(2)}, u32[]{:S(2)}) collective-permute-start(f32[32,512]{1,0:T(8,128)} %slice.104), channel_id=1, source_target_pairs={{0,2},{2,4},{4,6},{6,8},{8,10},{10,12},{12,14},{14,0},{1,3},{3,5},... | collective-permute-start | bytes 196616 | tf_op jit(solution)/shard_map/ppermute | solution.py:372
  36.3 10.5 %collective-permute-start.17 = (f32[32,512]{1,0:T(8,128)}, f32[32,512]{1,0:T(8,128)}, u32[]{:S(2)}, u32[]{:S(2)}) collective-permute-start(f32[32,512]{1,0:T(8,128)} %slice.105), channel_id=1, source_target_pairs={{0,14},{2,0},{4,2},{6,4},{8,6},{10,8},{12,10},{14,12},{1,15},{3,1}... | collective-permute-start | bytes 196616 | tf_op jit(solution)/shard_map/ppermute | solution.py:372
  39.6 6.6 %copy-start.2 = (f32[5,64,512]{2,1,0:T(8,128)S(1)}, f32[5,64,512]{2,1,0:T(8,128)}, u32[]{:S(2)}) copy-start(f32[5,64,512]{2,1,0:T(8,128)} %copy-done.1) | copy-start | bytes 1966084
  46.2 18.4 %collective-permute-start = (f32[8,64,512]{2,1,0:T(8,128)}, f32[8,64,512]{2,1,0:T(8,128)}, u32[]{:S(2)}, u32[]{:S(2)}) collective-permute-start(f32[8,64,512]{2,1,0:T(8,128)} %get-tuple-element.22), channel_id=1, source_target_pairs={{0,1},{1,0},{2,3},{3,2},{4,5},{5,4},{6,7},{7,6},{8,9},{9,8},{10,11... | collective-permute-start | bytes 3145736 | tf_op jit(solution)/shard_map/ppermute | solution.py:372
  46.2 4.4 %collective-permute-start.13 = (f32[5,64,512]{2,1,0:T(8,128)S(1)}, f32[5,64,512]{2,1,0:T(8,128)S(1)}, u32[]{:S(2)}, u32[]{:S(2)}) collective-permute-start(f32[5,64,512]{2,1,0:T(8,128)S(1)} %bitcast_dynamic-update-slice_fusion.near), channel_id=1, source_target_pairs={{0,1},{1,0},{2,3},{3,2},{4,5},{5,4},{6,7},{7,6},{8,9},{9,8},{10,11... | collective-permute-start | bytes 1966088 | tf_op jit(solution)/shard_map/ppermute | solution.py:372
  47.7 2.8 %collective-permute-start.18 = (f32[3,64,512]{2,1,0:T(8,128)S(1)}, f32[3,64,512]{2,1,0:T(8,128)S(1)}, u32[]{:S(2)}, u32[]{:S(2)}) collective-permute-start(f32[3,64,512]{2,1,0:T(8,128)S(1)} %pad_maximum_fusion.far), channel_id=1, source_target_pairs={{0,1},{1,0},{2,3},{3,2},{4,5},{5,4},{6,7},{7,6},{8,9},{9,8},{10,11... | collective-permute-start | bytes 1179656 | tf_op jit(solution)/shard_map/ppermute | solution.py:372
  56.0 1.3 copy-start
  57.4 39.6 %all-to-all-start.1 = ((f32[16,64,512]{2,1,0:T(8,128)}), f32[16,64,512]{2,1,0:T(8,128)S(1)}, u32[]{:S(2)}, u32[]{:S(2)}) async-start(f32[16,64,512]{2,1,0:T(8,128)} %bitcast.63), calls=%async_computation.1 | async-start | bytes 4194304 | tf_op jit(solution)/shard_map/all_to_all | solution.py:422
  66.1 7.5 %collective-permute-start.1 = (f32[32,512]{1,0:T(8,128)S(1)}, f32[32,512]{1,0:T(8,128)S(1)}, u32[]{:S(2)}, u32[]{:S(2)}) collective-permute-start(f32[32,512]{1,0:T(8,128)S(1)} %get-tuple-element.35), channel_id=1, source_target_pairs={{0,2},{2,4},{4,6},{6,8},{8,10},{10,12},{12,14},{14,0},{1,3},{3,5},... | collective-permute-start | bytes 196616 | tf_op jit(solution)/shard_map/ppermute | solution.py:372
  67.4 6.2 %collective-permute-start.5 = (f32[32,512]{1,0:T(8,128)S(1)}, f32[32,512]{1,0:T(8,128)S(1)}, u32[]{:S(2)}, u32[]{:S(2)}) collective-permute-start(f32[32,512]{1,0:T(8,128)S(1)} %get-tuple-element.36), channel_id=1, source_target_pairs={{0,14},{2,0},{4,2},{6,4},{8,6},{10,8},{12,10},{14,12},{1,15},{3,1}... | collective-permute-start | bytes 196616 | tf_op jit(solution)/shard_map/ppermute | solution.py:372
  73.6 6.3 %collective-permute-start.2 = (f32[64,512]{1,0:T(8,128)S(1)}, f32[64,512]{1,0:T(8,128)S(1)}, u32[]{:S(2)}, u32[]{:S(2)}) collective-permute-start(f32[64,512]{1,0:T(8,128)S(1)} %pad_maximum_fusion.1), channel_id=1, source_target_pairs={{0,2},{2,4},{4,6},{6,8},{8,10},{10,12},{12,14},{14,0},{1,3},{3,5},... | collective-permute-start | bytes 393224 | tf_op jit(solution)/shard_map/ppermute | solution.py:372
  73.7 6.3 %collective-permute-start.6 = (f32[64,512]{1,0:T(8,128)S(1)}, f32[64,512]{1,0:T(8,128)S(1)}, u32[]{:S(2)}, u32[]{:S(2)}) collective-permute-start(f32[64,512]{1,0:T(8,128)S(1)} %pad_maximum_fusion.2), channel_id=1, source_target_pairs={{0,14},{2,0},{4,2},{6,4},{8,6},{10,8},{12,10},{14,12},{1,15},{3,1}... | collective-permute-start | bytes 393224 | tf_op jit(solution)/shard_map/ppermute | solution.py:372
  80.0 6.3 %collective-permute-start.3 = (f32[64,512]{1,0:T(8,128)S(1)}, f32[64,512]{1,0:T(8,128)S(1)}, u32[]{:S(2)}, u32[]{:S(2)}) collective-permute-start(f32[64,512]{1,0:T(8,128)S(1)} %fusion.2), channel_id=1, source_target_pairs={{0,2},{2,4},{4,6},{6,8},{8,10},{10,12},{12,14},{14,0},{1,3},{3,5},... | collective-permute-start | bytes 393224 | tf_op jit(solution)/shard_map/ppermute | solution.py:372
  86.2 5.6 %collective-permute-start.7 = (f32[64,512]{1,0:T(8,128)S(1)}, f32[64,512]{1,0:T(8,128)S(1)}, u32[]{:S(2)}, u32[]{:S(2)}) collective-permute-start(f32[64,512]{1,0:T(8,128)S(1)} %get-tuple-element.32), channel_id=1, source_target_pairs={{0,14},{2,0},{4,2},{6,4},{8,6},{10,8},{12,10},{14,12},{1,15},{3,1}... | collective-permute-start | bytes 393224 | tf_op jit(solution)/shard_map/ppermute | solution.py:372
  87.1 6.3 %collective-permute-start.4 = (f32[64,512]{1,0:T(8,128)S(1)}, f32[64,512]{1,0:T(8,128)S(1)}, u32[]{:S(2)}, u32[]{:S(2)}) collective-permute-start(f32[64,512]{1,0:T(8,128)S(1)} %get-tuple-element.31), channel_id=1, source_target_pairs={{0,2},{2,4},{4,6},{6,8},{8,10},{10,12},{12,14},{14,0},{1,3},{3,5},... | collective-permute-start | bytes 393224 | tf_op jit(solution)/shard_map/ppermute | solution.py:372
  91.9 5.0 %collective-permute-start.8 = (f32[64,512]{1,0:T(8,128)S(1)}, f32[64,512]{1,0:T(8,128)S(1)}, u32[]{:S(2)}, u32[]{:S(2)}) collective-permute-start(f32[64,512]{1,0:T(8,128)S(1)} %fusion.1), channel_id=1, source_target_pairs={{0,14},{2,0},{4,2},{6,4},{8,6},{10,8},{12,10},{14,12},{1,15},{3,1}... | collective-permute-start | bytes 393224 | tf_op jit(solution)/shard_map/ppermute | solution.py:372
  99.5 27.8 %copy-start.3 = (f32[2,64,512]{2,1,0:T(8,128)}, f32[2,64,512]{2,1,0:T(8,128)S(1)}, u32[]{:S(2)}) copy-start(f32[2,64,512]{2,1,0:T(8,128)S(1)} %get-tuple-element.30.rows) | copy-start | bytes 786436
  99.5 2.9 %collective-permute-start.19 = (f32[2304,128]{1,0:T(8,128)S(1)}, f32[2304,128]{1,0:T(8,128)S(1)}, u32[]{:S(2)}, u32[]{:S(2)}) collective-permute-start(f32[2304,128]{1,0:T(8,128)S(1)} %get-tuple-element.24), channel_id=1, source_target_pairs={{0,1},{1,0},{2,3},{3,2},{4,5},{5,4},{6,7},{7,6},{8,9},{9,8},{10,11... | collective-permute-start | bytes 3538952 | tf_op jit(solution)/shard_map/ppermute | solution.py:372
  171.6 24.1 %collective-permute-start.20 = (f32[2304,128]{1,0:T(8,128)S(1)}, f32[2304,128]{1,0:T(8,128)S(1)}, u32[]{:S(2)}, u32[]{:S(2)}) collective-permute-start(f32[2304,128]{1,0:T(8,128)S(1)} %bitcast.65), channel_id=1, source_target_pairs={{0,1},{1,0},{2,3},{3,2},{4,5},{5,4},{6,7},{7,6},{8,9},{9,8},{10,11... | collective-permute-start | bytes 3538952 | tf_op jit(solution)/shard_map/ppermute | solution.py:372
